TPU v7x, 32 devices: a whole 2x2x4 slice. The times are simulated.
32 devices in a mesh: seq: 8 (over z, x), head: 4 (over y, core).
Axes of the slice: x: 2, y: 2, z: 4, core: 2. Of those that a mesh axis runs over, the one named last changes fastest.
Arguments:
- queries: bfloat16 [4096, 5120], P('seq', 'head'), may hold values from -13 to 13, as said below
- keys: bfloat16 [4096, 1024], P('seq', 'head'), may hold values from -13 to 13, as said below
- values: bfloat16 [4096, 1024], P('seq', 'head'), may hold values from -6 to 6
- out_weight: bfloat16 [5120, 2560], P('head', 'seq'), may hold values from -0.078125 to 0.078125
- d_proj: bfloat16 [4096, 2560], P('seq', 'head'), may hold values from -6 to 6
- block_section: int32 [32], replicated, may hold values from 0 to 3, as said below
- section_parent: int32 [4], replicated, may hold values from -1 to 2, as said below
- xref_owner: int32 [384, 1], P('seq'), may hold values from 0 to 7; in each aligned block of 48 rows (0 to 47, 48 to 95, ...) at most 6 rows name the same one
- xref_block: int32 [32, 12], P('seq'), may hold values from 0 to 3
- xref_valid: int32 [32, 12], P('seq'), may hold values 0 or 1
Outputs:
- projected: bfloat16 [4096, 2560], P('seq', 'head')
- d_queries: bfloat16 [4096, 5120], P('seq', 'head')
- d_keys: bfloat16 [4096, 1024], P('seq', 'head')
- d_values: bfloat16 [4096, 1024], P('seq', 'head')
Inputs may be any that keep to these rules, and one draw needn't show every extreme that they name: `queries`: entries of order one; a few rows of larger norm. `keys`: entries of order one; a few rows of larger norm. section_parent[s] is an earlier section for s > 0, and section_parent[0] = -1. `block_section`: sections are runs of consecutive blocks, 2 to 14 blocks each, some section exactly 14; no section begins at a block whose index is a positive multiple of 4. `xref_owner`: among the 48 rows of one device, no owner is named more than 6 times; some owner exactly 6 times.
All inputs are finite; a program needn't handle non-finite values. No bound on the sum of `xref_valid` on one device may be relied on, other than what follows from the above.
Results may differ from a plain program's by a relative error of at most 0.015.
The roundings to bfloat16 on the way count: a program that leaves them out, or rounds other values in their place, can miss the bound.
Values may be sent and summed in bfloat16 or wider, within the bound.
No kernel may reach another device: no remote copies, remote signals or barrier semaphores. Data moves between devices by JAX's collectives and lax.ppermute only.
A program may use at most 192 MiB of HBM per device.

v0:
```python
import jax
import jax.numpy as jnp
from jax import lax
from jax.sharding import PartitionSpec as P

HEAD_DIMENSION = 128
BLK = 128
LOOK = 4
ANC = 2
XREF = 12


neg_large = -1e30


def passed_along(block, axis, distance):
    devices = range(lax.axis_size(axis))
    route = [(i - distance, i) for i in devices if i - distance in devices]
    return lax.ppermute(block, axis, route)


def query_layout(block, kv_heads):
    row_count = block.shape[0]
    group_size = block.shape[1] // (HEAD_DIMENSION * kv_heads)
    return block.reshape(row_count, kv_heads, group_size, HEAD_DIMENSION)


def key_layout(key_set, kv_heads):
    num_blocks, row_count, key_value_width = key_set.shape
    return key_set.reshape(num_blocks * row_count, kv_heads, HEAD_DIMENSION)


def softmax_weights(scores, allowed):
    masked = jnp.where(allowed, scores, neg_large)
    row_max = jnp.max(masked, axis=-1, keepdims=True)
    exponent = jnp.where(allowed, jnp.exp(masked - row_max), 0.0)
    return exponent / jnp.sum(exponent, axis=-1, keepdims=True)


def product(form, left, right):
    return jnp.einsum(form, left, right, preferred_element_type=jnp.float32)


def forward_block(query_block, key_set, value_set, allowed):
    kv_heads = key_set.shape[2] // HEAD_DIMENSION
    scaling = HEAD_DIMENSION ** (-0.5)
    query_heads = query_layout(query_block, kv_heads)
    key_heads = key_layout(key_set, kv_heads)
    value_heads = key_layout(value_set, kv_heads)
    scores = product("qcgd,kcd->cqgk", query_heads, key_heads) * scaling
    weights = softmax_weights(scores, allowed[None, :, None, :])
    output = product("cqgk,kcd->qcgd", weights.astype(jnp.bfloat16), value_heads)
    return output.reshape(query_block.shape[0], -1).astype(jnp.bfloat16)


def backward_block(query_block, key_set, value_set, allowed, attn, d_attn):
    kv_heads = key_set.shape[2] // HEAD_DIMENSION
    scaling = HEAD_DIMENSION ** (-0.5)
    num_blocks = key_set.shape[0]
    row_count = query_block.shape[0]
    query_heads = query_layout(query_block, kv_heads)
    key_heads = key_layout(key_set, kv_heads)
    value_heads = key_layout(value_set, kv_heads)
    scores = product("qcgd,kcd->cqgk", query_heads, key_heads) * scaling
    weights = softmax_weights(scores, allowed[None, :, None, :])
    light = weights.astype(jnp.bfloat16)
    grad_heads = query_layout(d_attn, kv_heads)
    attn_heads = query_layout(attn, kv_heads)
    delta = jnp.einsum(
        "qcgd,qcgd->cqg", grad_heads.astype(jnp.float32), attn_heads.astype(jnp.float32)
    )[..., None]
    d_weights = product("qcgd,kcd->cqgk", grad_heads, value_heads)
    d_scores = (weights * (d_weights - delta) * scaling).astype(jnp.bfloat16)
    grad_query = product("cqgk,kcd->qcgd", d_scores, key_heads)
    key_terms = product("cqgk,qcgd->kcd", d_scores, query_heads)
    value_terms = product("cqgk,qcgd->kcd", light, grad_heads)
    return (
        grad_query.reshape(row_count, -1).astype(jnp.bfloat16),
        key_terms.reshape(num_blocks, -1),
        value_terms.reshape(num_blocks, -1),
    )


def run_forward(operands):
    return forward_block(operands[0], operands[1], operands[2], operands[3])


def run_backward(operands):
    return backward_block(
        operands[0], operands[1], operands[2], operands[3], operands[4], operands[5]
    )


def on_device(
    queries,
    keys,
    values,
    out_weight,
    d_proj,
    block_section,
    section_parent,
    xref_owner,
    xref_block,
    xref_valid,
):
    seq_count = lax.axis_size("seq")
    seq_rank = lax.axis_index("seq")
    tok_local = queries.shape[0]
    blk_count = tok_local // BLK
    key_value_width = keys.shape[1]
    blk_width = BLK * key_value_width
    sections = section_parent.shape[0]
    behind = LOOK - 1
    key_count = LOOK + ANC + XREF
    first_blk = seq_rank * blk_count
    key_flat = keys.reshape(blk_count, blk_width)
    value_flat = values.reshape(blk_count, blk_width)
    section_ids = jnp.arange(sections, dtype=jnp.int32)
    my_sec = lax.dynamic_slice_in_dim(block_section, first_blk, blk_count)
    counts = jnp.sum((block_section[:, None] == section_ids[None, :]).astype(jnp.float32), axis=0)
    root_counts = jnp.sqrt(counts)
    mine = (section_ids[:, None] == my_sec[None, :]).astype(jnp.float32)
    chain = [my_sec]
    prior = chain[-1]
    chain.append(
        jnp.where(
            prior >= 0,
            jnp.sum(
                jnp.where(prior[:, None] == section_ids[None, :], section_parent[None, :], 0),
                axis=1,
            ),
            -1,
        )
    )
    ancestors = jnp.stack(chain, axis=1).reshape(-1)
    chosen_up = ancestors[:, None] == section_ids[None, :]
    prev_keys, prev_values = passed_along(
        (keys[tok_local - behind * BLK :], values[tok_local - behind * BLK :]), "seq", 1
    )
    extended_keys = jnp.concatenate([prev_keys, keys], axis=0).reshape(
        blk_count + behind, BLK, key_value_width
    )
    extended_values = jnp.concatenate([prev_values, values], axis=0).reshape(
        blk_count + behind, BLK, key_value_width
    )
    mine_light = mine.astype(jnp.bfloat16)
    part_keys = (
        jnp.dot(mine_light, key_flat, preferred_element_type=jnp.float32) / root_counts[:, None]
    )
    part_values = (
        jnp.dot(mine_light, value_flat, preferred_element_type=jnp.float32) / root_counts[:, None]
    )
    total_keys, total_values = (
        lax.psum(part_keys.astype(jnp.bfloat16), "seq").astype(jnp.float32),
        lax.psum(part_values.astype(jnp.bfloat16), "seq").astype(jnp.float32),
    )
    summary_keys = total_keys.astype(jnp.bfloat16)
    summary_values = total_values.astype(jnp.bfloat16)
    chosen_light = chosen_up.astype(jnp.bfloat16)
    up_keys = (
        jnp.dot(chosen_light, summary_keys, preferred_element_type=jnp.float32)
        .astype(jnp.bfloat16)
        .reshape(blk_count, ANC, BLK, key_value_width)
    )
    up_values = (
        jnp.dot(chosen_light, summary_values, preferred_element_type=jnp.float32)
        .astype(jnp.bfloat16)
        .reshape(blk_count, ANC, BLK, key_value_width)
    )
    owners = xref_owner.reshape(-1)
    wanted = xref_block.reshape(-1)
    slot_total = owners.shape[0]
    slot_cap = max(2, slot_total // seq_count)
    slot_order = jnp.arange(slot_total)
    slot_rank = jnp.sum(
        (owners[:, None] == owners[None, :]) & (slot_order[:, None] > slot_order[None, :]), axis=1
    )
    placed = (owners * slot_cap + slot_rank)[:, None] == jnp.arange(seq_count * slot_cap)[None, :]
    placed_light = placed.astype(jnp.bfloat16)
    request = jnp.sum(jnp.where(placed, wanted[:, None] + 1, 0), axis=0).reshape(
        seq_count, slot_cap
    )
    asked_for = lax.all_to_all(request, "seq", split_axis=0, concat_axis=0, tiled=True).reshape(-1)
    served = ((asked_for - 1)[:, None] == jnp.arange(blk_count)[None, :]).astype(jnp.bfloat16)
    all_keys, all_values = (
        lax.all_gather(keys, "seq", axis=0, tiled=True),
        lax.all_gather(values, "seq", axis=0, tiled=True),
    )
    picked = (
        (owners * blk_count + wanted)[:, None] == jnp.arange(blk_count * seq_count)[None, :]
    ).astype(jnp.bfloat16)
    ref_keys = jnp.dot(
        picked,
        all_keys.reshape(blk_count * seq_count, blk_width),
        preferred_element_type=jnp.float32,
    )
    ref_values = jnp.dot(
        picked,
        all_values.reshape(blk_count * seq_count, blk_width),
        preferred_element_type=jnp.float32,
    )
    ref_keys = ref_keys.astype(jnp.bfloat16).reshape(blk_count, XREF, BLK, key_value_width)
    ref_values = ref_values.astype(jnp.bfloat16).reshape(blk_count, XREF, BLK, key_value_width)
    window_keys = jnp.stack(
        [extended_keys[offset : offset + blk_count] for offset in range(LOOK)], axis=1
    )
    window_values = jnp.stack(
        [extended_values[offset : offset + blk_count] for offset in range(LOOK)], axis=1
    )
    key_sets = jnp.concatenate([window_keys, up_keys, ref_keys], axis=1)
    value_sets = jnp.concatenate([window_values, up_values, ref_values], axis=1)
    positions = jnp.arange(BLK)
    causal = positions[None, :] <= positions[:, None]
    is_last = jnp.arange(LOOK) == LOOK - 1
    padded_sec = jnp.concatenate([jnp.full((behind,), -1, jnp.int32), block_section])
    extended_sec = lax.dynamic_slice_in_dim(padded_sec, first_blk, blk_count + behind)
    window_sec = jnp.stack(
        [extended_sec[offset : offset + blk_count] for offset in range(LOOK)], axis=1
    )
    own_ok = window_sec == my_sec[:, None]
    own_allowed = own_ok[:, None, :, None] & (
        jnp.logical_not(is_last)[None, None, :, None] | causal[None, :, None, :]
    )
    up_allowed = jnp.broadcast_to(
        (ancestors >= 0).reshape(blk_count, ANC)[:, None, :, None], (blk_count, BLK, ANC, BLK)
    )
    ref_allowed = jnp.broadcast_to((xref_valid > 0)[:, None, :, None], (blk_count, BLK, XREF, BLK))
    allowed = jnp.concatenate([own_allowed, up_allowed, ref_allowed], axis=2).reshape(
        blk_count, BLK, key_count * BLK
    )
    query_blocks = queries.reshape(blk_count, BLK, -1)
    attn_blocks = lax.map(run_forward, (query_blocks, key_sets, value_sets, allowed))
    attn = attn_blocks.reshape(tok_local, -1)
    d_full = lax.all_gather(d_proj, "head", axis=1, tiled=True)
    partials = jnp.dot(
        attn,
        lax.all_gather(out_weight, "seq", axis=1, tiled=True),
        preferred_element_type=jnp.float32,
    )
    d_attn = lax.dot_general(
        d_full,
        lax.all_gather(out_weight, "seq", axis=1, tiled=True),
        (((1,), (1,)), ((), ())),
        preferred_element_type=jnp.float32,
    ).astype(jnp.bfloat16)
    projected = lax.psum_scatter(
        partials.astype(jnp.bfloat16), "head", scatter_dimension=1, tiled=True
    )
    grad_queries, key_terms, value_terms = lax.map(
        run_backward,
        (
            query_blocks,
            key_sets,
            value_sets,
            allowed,
            attn_blocks,
            d_attn.reshape(blk_count, BLK, -1),
        ),
    )

    def spread(terms):
        extended = jnp.zeros((blk_count + behind, blk_width), jnp.float32)
        for offset in range(LOOK):
            extended = extended.at[offset : offset + blk_count].add(terms[:, offset])
        return extended

    extended_dk = spread(key_terms)
    extended_dv = spread(value_terms)
    next_dk, next_dv = (
        passed_along(extended_dk[:behind].astype(jnp.bfloat16), "seq", -1).astype(jnp.float32),
        passed_along(extended_dv[:behind].astype(jnp.bfloat16), "seq", -1).astype(jnp.float32),
    )
    own_dk = extended_dk[behind:] + jnp.pad(next_dk, ((blk_count - behind, 0), (0, 0)))
    own_dv = extended_dv[behind:] + jnp.pad(next_dv, ((blk_count - behind, 0), (0, 0)))
    chosen_float = chosen_up.T.astype(jnp.float32)
    section_dk = jnp.dot(
        chosen_float,
        key_terms[:, LOOK : LOOK + ANC].reshape(blk_count * ANC, blk_width),
        precision=lax.Precision.HIGHEST,
    )
    section_dv = jnp.dot(
        chosen_float,
        value_terms[:, LOOK : LOOK + ANC].reshape(blk_count * ANC, blk_width),
        precision=lax.Precision.HIGHEST,
    )
    summed_dk, summed_dv = (
        lax.psum(section_dk.astype(jnp.bfloat16), "seq").astype(jnp.float32),
        lax.psum(section_dv.astype(jnp.bfloat16), "seq").astype(jnp.float32),
    )
    spread_down = (mine / root_counts[:, None]).T
    up_dk = jnp.dot(spread_down, summed_dk, precision=lax.Precision.HIGHEST)
    up_dv = jnp.dot(spread_down, summed_dv, precision=lax.Precision.HIGHEST)
    slot_dk_light = (
        key_terms[:, LOOK + ANC :].reshape(blk_count * XREF, blk_width).astype(jnp.bfloat16)
    )
    slot_dv_light = (
        value_terms[:, LOOK + ANC :].reshape(blk_count * XREF, blk_width).astype(jnp.bfloat16)
    )
    placed_back = placed_light.T
    slot_dk = (
        jnp.dot(placed_back, slot_dk_light, preferred_element_type=jnp.float32)
        .astype(jnp.bfloat16)
        .reshape(seq_count, slot_cap, blk_width)
    )
    slot_dv = (
        jnp.dot(placed_back, slot_dv_light, preferred_element_type=jnp.float32)
        .astype(jnp.bfloat16)
        .reshape(seq_count, slot_cap, blk_width)
    )
    back_dk, back_dv = (
        lax.all_to_all(slot_dk, "seq", split_axis=0, concat_axis=0, tiled=True),
        lax.all_to_all(slot_dv, "seq", split_axis=0, concat_axis=0, tiled=True),
    )
    served_back = served.T
    ref_dk = jnp.dot(
        served_back,
        back_dk.reshape(seq_count * slot_cap, blk_width),
        preferred_element_type=jnp.float32,
    )
    ref_dv = jnp.dot(
        served_back,
        back_dv.reshape(seq_count * slot_cap, blk_width),
        preferred_element_type=jnp.float32,
    )
    d_keys = (own_dk + up_dk + ref_dk).astype(jnp.bfloat16).reshape(tok_local, key_value_width)
    d_values = (own_dv + up_dv + ref_dv).astype(jnp.bfloat16).reshape(tok_local, key_value_width)
    return (projected, grad_queries.reshape(tok_local, -1), d_keys, d_values)


def solution(mesh):
    placed = (
        P("seq", "head"),
        P("seq", "head"),
        P("seq", "head"),
        P("head", "seq"),
        P("seq", "head"),
        P(),
        P(),
        P("seq", None),
        P("seq", None),
        P("seq", None),
    )
    return jax.shard_map(
        on_device,
        mesh=mesh,
        in_specs=placed,
        out_specs=(P("seq", "head"), P("seq", "head"), P("seq", "head"), P("seq", "head")),
        check_vma=False,
    )
```

profile of v0, /device:TPU:0, one launch (start us, length us, event | category | flops | bytes accessed | tf_op | source)
XLA Modules:
  0.0 916.1 jit_solution(16726008169949510569)
XLA Ops:
  15.9 5.5 collective-permute-start
  45.3 45.7 %all-reduce.12.cloned.1.call-done = (bf16[4,32768]{1,0:T(4,128)(2,1)}, bf16[4,32768]{1,0:T(4,128)(2,1)}) async-done(((bf16[4,32768]{1,0:T(4,128)(2,1)}, bf16[4,32768]{1,0:T(4,128)(2,1)}), (bf16[4,32768]{1,0:T(4,128)(2,1)}, bf16[4,32768]{1,0:T(4,128)(2,1)})) %all-reduce.12.cloned.1.call-update) | async-done | bytes 524304 | tf_op jit(solution)/shard_map/psum | solution.py:155
  95.5 45.9 %all-gather.5.cloned.1.call-done = bf16[4096,256]{1,0:T(8,128)(2,1)} async-done(((bf16[512,256]{1,0:T(8,128)(2,1)}), bf16[4096,256]{1,0:T(8,128)(2,1)}) %all-gather.5.cloned.1.call-update) | async-done | bytes 2097168 | tf_op jit(solution)/shard_map/all_gather | solution.py:187
  146.0 45.1 %all-gather.7.cloned.1.call-done = bf16[4096,256]{1,0:T(8,128)(2,1)} async-done(((bf16[512,256]{1,0:T(8,128)(2,1)}), bf16[4096,256]{1,0:T(8,128)(2,1)}) %all-gather.7.cloned.1.call-update) | async-done | bytes 2097168 | tf_op jit(solution)/shard_map/all_gather | solution.py:186
  202.0 95.5 %while.32 = (s32[]{:T(128)}, bf16[4,128,1280]{1,2,0:T(8,128)(2,1)}, bf16[4,18,128,256]{3,2,1,0:T(8,128)(2,1)}, pred[4,128,2304]{2,1,0:T(8,128)(4,1)}, bf16[4,128...) while((s32[]{:T(128)}, bf16[4,128,1280]{1,2,0:T(8,128)(2,1)}, ...), condition=%wide.region_7.8_spmd, body=%wide.region_4.0_spmd.sunk | while | flops 1530759424 | bytes 38250596 | solution.py:232
  207.8 10.7 %fusion.123 = (f32[2,128,5]{1,2,0:T(8,128)S(1)}, f32[2,128,5,2304]{3,1,2,0:T(8,128)}) fusion(pred[128,2304]{1,0:T(8,128)(4,1)} %dynamic-slice_bitcast_fusion.5, bf16[128,2,5,128]{0,3,2,1:T(8,128)(2,1)} %bitcast.225, bf16[2304,2,128,1]{2,1,0,3:T(2,128)(2,1)S(1)} %bitcast.217), kind=kOutput, calls=%fused_computation.159.clone.1 | convolution fusion | flops 769722624 | bytes 13603840 | tf_op jit(solution)/shard_map/while/body/eval_jaxpr/sub | solution.py:36
  218.8 6.4 fusion.124
  231.6 10.7 %fusion.123 = (f32[2,128,5]{1,2,0:T(8,128)S(1)}, f32[2,128,5,2304]{3,1,2,0:T(8,128)}) fusion(pred[128,2304]{1,0:T(8,128)(4,1)} %dynamic-slice_bitcast_fusion.5, bf16[128,2,5,128]{0,3,2,1:T(8,128)(2,1)} %bitcast.225, bf16[2304,2,128,1]{2,1,0,3:T(2,128)(2,1)S(1)} %bitcast.217), kind=kOutput, calls=%fused_computation.159.clone.1 | convolution fusion | flops 769722624 | bytes 13603840 | tf_op jit(solution)/shard_map/while/body/eval_jaxpr/sub | solution.py:36
  242.5 6.5 fusion.124
  255.3 10.9 %fusion.123 = (f32[2,128,5]{1,2,0:T(8,128)S(1)}, f32[2,128,5,2304]{3,1,2,0:T(8,128)}) fusion(pred[128,2304]{1,0:T(8,128)(4,1)} %dynamic-slice_bitcast_fusion.5, bf16[128,2,5,128]{0,3,2,1:T(8,128)(2,1)} %bitcast.225, bf16[2304,2,128,1]{2,1,0,3:T(2,128)(2,1)S(1)} %bitcast.217), kind=kOutput, calls=%fused_computation.159.clone.1 | convolution fusion | flops 769722624 | bytes 13603840 | tf_op jit(solution)/shard_map/while/body/eval_jaxpr/sub | solution.py:36
  266.5 6.5 fusion.124
  279.3 10.7 %fusion.123 = (f32[2,128,5]{1,2,0:T(8,128)S(1)}, f32[2,128,5,2304]{3,1,2,0:T(8,128)}) fusion(pred[128,2304]{1,0:T(8,128)(4,1)} %dynamic-slice_bitcast_fusion.5, bf16[128,2,5,128]{0,3,2,1:T(8,128)(2,1)} %bitcast.225, bf16[2304,2,128,1]{2,1,0,3:T(2,128)(2,1)S(1)} %bitcast.217), kind=kOutput, calls=%fused_computation.159.clone.1 | convolution fusion | flops 769722624 | bytes 13603840 | tf_op jit(solution)/shard_map/while/body/eval_jaxpr/sub | solution.py:36
  290.2 6.5 fusion.124
  299.9 20.7 %all-gather.9.cloned.1.call-done = bf16[1280,2560]{0,1:T(8,128)(2,1)} async-done(((bf16[1280,320]{0,1:T(8,128)(2,1)}), bf16[1280,2560]{0,1:T(8,128)(2,1)}) %all-gather.9.cloned.1.call-update) | async-done | bytes 6553616 | tf_op jit(solution)/shard_map/all_gather | solution.py:237
  320.6 8.3 convolution_convert_fusion.10
  328.9 252.5 %while.33 = (s32[]{:T(128)}, bf16[4,128,1280]{2,1,0:T(8,128)(2,1)}, f32[4,18,32768]{2,1,0:T(8,128)}, f32[4,18,32768]{2,1,0:T(8,128)}, bf16[4,18,128,256]{3,2,1,0...) while((s32[]{:T(128)}, bf16[4,128,1280]{2,1,0:T(8,128)(2,1)}, ...), condition=%wide.region_12.13_spmd, body=%wide.region_9.12_spmd.sunk | while | flops 3811083264 | bytes 134538416 | solution.py:249
  336.8 8.3 fusion.136
  347.5 7.6 multiply_convert_fusion.2
  399.7 8.3 fusion.136
  410.5 7.6 multiply_convert_fusion.2
  462.6 8.3 fusion.136
  473.4 7.6 multiply_convert_fusion.2
  525.7 8.3 fusion.136
  536.5 7.6 multiply_convert_fusion.2
  584.0 14.2 %copy.134 = f32[4,18,32768]{2,0,1:T(4,128)} copy(f32[4,18,32768]{2,1,0:T(8,128)} %get-tuple-element.188) | data formatting | bytes 18874368 | tf_op jit(solution)/shard_map/while | solution.py:249
  598.2 7.2 slice.345
  608.1 14.5 %copy.139 = f32[4,18,32768]{2,0,1:T(4,128)} copy(f32[4,18,32768]{2,1,0:T(8,128)} %get-tuple-element.189) | data formatting | bytes 18874368 | tf_op jit(solution)/shard_map/while | solution.py:249
  622.6 7.5 slice.344
  630.1 7.7 convolution_convert_fusion.9
  686.9 84.2 %all-to-all-done.1 = bf16[8,6,32768]{2,1,0:T(8,128)(2,1)} async-done(((bf16[8,6,32768]{2,1,0:T(8,128)(2,1)}), bf16[8,6,32768]{2,1,0:T(8,128)(2,1)}, u32[]{:S(2)}, u32[]{:S(2)}) %all-to-all-start.1) | async-done | bytes 3145760 | tf_op jit(solution)/shard_map/all_to_all | solution.py:311
  780.9 76.7 %all-reduce.10.cloned.1.call-done = (bf16[4,32768]{1,0:T(4,128)(2,1)}, bf16[4,32768]{1,0:T(4,128)(2,1)}) async-done(((bf16[4,32768]{1,0:T(4,128)(2,1)}, bf16[4,32768]{1,0:T(4,128)(2,1)}), (bf16[4,32768]{1,0:T(4,128)(2,1)}, bf16[4,32768]{1,0:T(4,128)(2,1)})) %all-reduce.10.cloned.1.call-update) | async-done | bytes 524304 | tf_op jit(solution)/shard_map/psum | solution.py:287
  862.6 31.7 %reduce-scatter.4.cloned.1.call-done = bf16[640,512]{1,0:T(8,128)(2,1)} async-done(((bf16[2560,512]{1,0:T(8,128)(2,1)}), bf16[640,512]{1,0:T(8,128)(2,1)}) %reduce-scatter.4.cloned.1.call-update) | async-done | bytes 655376
  (295 shorter events, 352.6 us)
Async XLA Ops:
  7.2 83.8 %all-reduce.12.cloned.1.call-start = ((), (), s32[]{:S(2)}) async-start(), calls=%async_computation.10 | async-start | bytes 1048576 | tf_op jit(solution)/shard_map/psum | solution.py:155
  9.9 21.5 %copy-start.15 = (s32[4]{0:T(128)}, s32[4]{0:T(128)S(1)}, u32[]{:S(2)}) copy-start(s32[4]{0:T(128)S(1)} %dynamic_slice.39) | copy-start | bytes 52
  11.0 4.1 copy-start.4
  11.0 10.4 %copy-start.5 = (bf16[512,256]{1,0:T(8,128)(2,1)S(1)}, bf16[512,256]{1,0:T(8,128)(2,1)}, u32[]{:S(2)}) copy-start(bf16[512,256]{1,0:T(8,128)(2,1)} %param.31) | copy-start | bytes 786436
  11.1 13.2 %copy-start.11 = (s32[4,12]{1,0:T(4,128)S(1)}, s32[4,12]{1,0:T(4,128)}, u32[]{:S(2)}) copy-start(s32[4,12]{1,0:T(4,128)} %param.38) | copy-start | bytes 580
  11.1 13.3 %copy-start.20 = (s32[48,1]{0,1:T(1,128)S(1)}, s32[48,1]{0,1:T(1,128)}, u32[]{:S(2)}) copy-start(s32[48,1]{0,1:T(1,128)} %param.37) | copy-start | bytes 580
  12.1 18.7 %copy-start.21 = (s32[32]{0:T(128)S(1)}, s32[32]{0:T(128)}, u32[]{:S(2)}) copy-start(s32[32]{0:T(128)} %param.35) | copy-start | bytes 388
  12.1 18.9 %copy-start.22 = (s32[4]{0:T(128)S(1)}, s32[4]{0:T(128)}, u32[]{:S(2)}) copy-start(s32[4]{0:T(128)} %param.36) | copy-start | bytes 52
  12.1 19.0 %copy-start.19 = (s32[4,12]{1,0:T(4,128)S(1)}, s32[4,12]{1,0:T(4,128)}, u32[]{:S(2)}) copy-start(s32[4,12]{1,0:T(4,128)} %param.39) | copy-start | bytes 580
  13.1 128.3 %all-gather.5.cloned.1.call-start = ((), (), s32[]{:S(2)}) async-start(), calls=%async_computation.4 | async-start | bytes 2359296 | tf_op jit(solution)/shard_map/all_gather | solution.py:187
  13.8 177.3 %all-gather.7.cloned.1.call-start = ((), (), s32[]{:S(2)}) async-start(), calls=%async_computation.5 | async-start | bytes 2359296 | tf_op jit(solution)/shard_map/all_gather | solution.py:186
  14.6 285.3 %all-gather.11.cloned.1.call-start = ((), (), s32[]{:S(2)}) async-start(), calls=%async_computation.7 | async-start | bytes 3276800 | tf_op jit(solution)/shard_map/all_gather | solution.py:234
  15.9 22.4 %collective-permute-start = (bf16[384,256]{1,0:T(8,128)(2,1)}, bf16[384,256]{1,0:T(8,128)(2,1)}, u32[]{:S(2)}, u32[]{:S(2)}) collective-permute-start(bf16[384,256]{1,0:T(8,128)(2,1)} %slice.240), channel_id=1, source_target_pairs={{0,4},{4,8},{8,12},{12,16},{16,20},{20,24},{24,28},{1,5},{5,9},{9,... | collective-permute-start | bytes 589832 | tf_op jit(solution)/shard_map/ppermute | solution.py:19
  21.4 18.6 %collective-permute-start.1 = (bf16[384,256]{1,0:T(8,128)(2,1)S(1)}, bf16[384,256]{1,0:T(8,128)(2,1)S(1)}, u32[]{:S(2)}, u32[]{:S(2)}) collective-permute-start(bf16[384,256]{1,0:T(8,128)(2,1)S(1)} %slice.248), channel_id=1, source_target_pairs={{0,4},{4,8},{8,12},{12,16},{16,20},{20,24},{24,28},{1,5},{5,9},{9,... | collective-permute-start | bytes 589832 | tf_op jit(solution)/shard_map/ppermute | solution.py:19
  25.4 12.2 %all-to-all-start = ((s32[8,1,6]{2,1,0:T(1,128)}), s32[8,1,6]{2,1,0:T(1,128)S(1)}, u32[]{:S(2)}, u32[]{:S(2)}) async-start(s32[8,1,6]{2,1,0:T(1,128)} %bitcast.52), calls=%async_computation | async-start | bytes 8192 | tf_op jit(solution)/shard_map/all_to_all | solution.py:183
  30.2 290.4 %all-gather.9.cloned.1.call-start = ((), (), s32[]{:S(2)}) async-start(), calls=%async_computation.6 | async-start | bytes 7372800 | tf_op jit(solution)/shard_map/all_gather | solution.py:237
  32.5 59.9 %copy-start.9 = (s32[8]{0:T(128)}, s32[8]{0:T(128)S(1)}, u32[]{:S(2)}) copy-start(s32[8]{0:T(128)S(1)} %eq.130) | copy-start | bytes 100
  622.6 7.5 copy-start.8
  637.8 5.2 copy-start.10
  653.5 4.9 copy-start.13
  654.4 244.9 %collective-permute-start.2 = (bf16[3,32768]{1,0:T(4,128)(2,1)S(1)}, bf16[3,32768]{1,0:T(4,128)(2,1)}, u32[]{:S(2)}, u32[]{:S(2)}) collective-permute-start(bf16[3,32768]{1,0:T(4,128)(2,1)S(1)} %slice.347), channel_id=1, source_target_pairs={{4,0},{8,4},{12,8},{16,12},{20,16},{24,20},{28,24},{5,1},{9,5},{13... | collective-permute-start | bytes 589832 | tf_op jit(solution)/shard_map/ppermute | solution.py:19
  665.2 106.0 %all-to-all-start.1 = ((bf16[8,6,32768]{2,1,0:T(8,128)(2,1)}), bf16[8,6,32768]{2,1,0:T(8,128)(2,1)}, u32[]{:S(2)}, u32[]{:S(2)}) async-start(bf16[8,6,32768]{2,1,0:T(8,128)(2,1)} %reshape.496), calls=%async_computation.1 | async-start | bytes 8388608 | tf_op jit(solution)/shard_map/all_to_all | solution.py:311
  670.7 186.8 %all-reduce.10.cloned.1.call-start = ((), (), s32[]{:S(2)}) async-start(), calls=%async_computation.9 | async-start | bytes 1048576 | tf_op jit(solution)/shard_map/psum | solution.py:287
  671.3 223.0 %reduce-scatter.4.cloned.1.call-start = ((), (), s32[]{:S(2)}) async-start(), calls=%async_computation.8 | async-start | bytes 3276800
  679.9 4.1 copy-start.7
  679.9 5.3 copy-start.1
  686.9 170.6 %copy-start.16 = (s32[4]{0:T(128)S(1)}, s32[4]{0:T(128)}, u32[]{:S(2)}) copy-start(s32[4]{0:T(128)} %copy-done.15) | copy-start | bytes 52
  686.9 170.6 %copy-start.18 = (f32[4]{0:T(128)S(1)}, f32[4]{0:T(128)}, u32[]{:S(2)}) copy-start(f32[4]{0:T(128)} %copy-done.17) | copy-start | bytes 52
  771.2 131.5 %all-to-all-start.2 = ((bf16[8,6,32768]{2,1,0:T(8,128)(2,1)}), bf16[8,6,32768]{2,1,0:T(8,128)(2,1)}, u32[]{:S(2)}, u32[]{:S(2)}) async-start(bf16[8,6,32768]{2,1,0:T(8,128)(2,1)} %reshape.503), calls=%async_computation.2 | async-start | bytes 8388608 | tf_op jit(solution)/shard_map/all_to_all | solution.py:312
  778.7 115.7 %copy-start.2 = (f32[7,32768]{1,0:T(8,128)}, f32[7,32768]{1,0:T(8,128)S(1)}, u32[]{:S(2)}) copy-start(f32[7,32768]{1,0:T(8,128)S(1)} %scatter-add.29) | copy-start | bytes 2752516
  779.6 125.9 %collective-permute-start.3 = (bf16[3,32768]{1,0:T(4,128)(2,1)}, bf16[3,32768]{1,0:T(4,128)(2,1)}, u32[]{:S(2)}, u32[]{:S(2)}) collective-permute-start(bf16[3,32768]{1,0:T(4,128)(2,1)} %slice.346), channel_id=1, source_target_pairs={{4,0},{8,4},{12,8},{16,12},{20,16},{24,20},{28,24},{5,1},{9,5},{13... | collective-permute-start | bytes 589832 | tf_op jit(solution)/shard_map/ppermute | solution.py:19
  894.3 5.0 copy-start.14
  (8 other events, 16.5 us)
Sparse Core Ops, SparseCore 0:
  13.2 77.6 all-reduce.11
  93.1 48.2 all-gather.4
  143.5 47.6 all-gather.6
  192.6 24.0 all-gather.10
  218.7 101.8 all-gather.8
  675.3 182.2 all-reduce.9
  860.1 34.2 reduce-scatter.3
where the time goes:
time: 927 us; the launch traced here: 916 us
  waiting for transfers between devices  353 us (38%)
  local copies, waits for them, and re-layouts  290 us (31%)
  matrix products  224 us (24%)
  starting transfers between devices  26.1 us (3%)
  between operations  15.2 us (2%)
    dot_general x20, matrix products, product(): return jnp.einsum(form, left, right, preferred_element_type=jnp.float32)  105 us
    all_to_all x1, waiting for transfers between devices, on_device(): lax.all_to_all(slot_dk, 'seq', split_axis=0, concat_axis=0, tiled=True)  84.2 us
    psum x1, waiting for transfers between devices, on_device(): lax.psum(section_dk.astype(jnp.bfloat16), 'seq').astype(jnp.float32)  76.7 us
    sub x8, matrix products, softmax_weights(): exponent = jnp.where(allowed, jnp.exp(masked - row_max), 0.0)  75.9 us
    all_gather x1, waiting for transfers between devices, on_device(): lax.all_gather(values, 'seq', axis=0, tiled=True)  45.9 us
    psum x1, waiting for transfers between devices, on_device(): lax.psum(part_values.astype(jnp.bfloat16), 'seq').astype(jnp.float32)  45.7 us
    all_gather x1, waiting for transfers between devices, on_device(): lax.all_gather(keys, 'seq', axis=0, tiled=True)  45.1 us
    dynamic_slice x32, local copies, waits for them, and re-layouts, on_device(): lax.map(run_forward, (query_blocks, key_sets, value_sets, allowed))  37.7 us
  transfers between devices with their start and end apart: 14, of which 7 were waited for; matrix products, arithmetic and copies ran while one was open for 19% of the time, Pallas kernels for 0%

commit v1 on v0

v1 whole, which is shorter than its diff:
```python
import functools
import math

import jax
import jax.numpy as jnp
from jax import lax
from jax.experimental import pallas as pl
from jax.experimental.pallas import tpu as pltpu
from jax.sharding import PartitionSpec as P

HEAD_DIMENSION = 128
BLK = 128
LOOK = 4
ANC = 2
XREF = 12
SLOTS = LOOK + ANC + XREF
GROUP = 2

neg_large = -1e30
scaling = HEAD_DIMENSION ** (-0.5)
to_base_two = scaling * math.log2(math.e)
vmem_limit = 62 * 1024 * 1024


def rows_of(index):
    return pl.ds(pl.multiple_of(index * BLK, BLK), BLK)


def product(left, right, left_dim, right_dim):
    return lax.dot_general(
        left, right, (((left_dim,), (right_dim,)), ((), ())), preferred_element_type=jnp.float32
    )


def stacked(block_ref, heads):
    return [block_ref[:, g * HEAD_DIMENSION : (g + 1) * HEAD_DIMENSION] for g in range(heads)]


def masked_scores(scores, first_slot, valid_count, heads):
    rows = heads * BLK
    key_minus_query = lax.broadcasted_iota(jnp.int32, (BLK, BLK), 1) - lax.broadcasted_iota(
        jnp.int32, (BLK, BLK), 0
    )
    ahead = jnp.concatenate([key_minus_query] * heads, axis=0)
    pieces = []
    for w in range(GROUP):
        slot = first_slot + w
        reach = jnp.where(slot < valid_count, jnp.where(slot == 0, 0, BLK), -BLK)
        piece = scores[:, w * BLK : (w + 1) * BLK]
        pieces.append(jnp.where(ahead <= reach, piece, neg_large))
    return pieces


def forward_kernel(
    order_ref, count_ref, section_ref, root_ref,
    query_ref, key_ref, value_ref,
    attn_ref, lse_ref, all_keys_ref, all_values_ref,
    stack_ref, score_ref, wide_ref, out_ref, total_ref,
):
    block = pl.program_id(1)
    heads = query_ref.shape[1] // HEAD_DIMENSION
    blocks = key_ref.shape[0] // BLK
    sections = root_ref.shape[0]

    @pl.when(block == 0)
    def _():
        for source, target in ((key_ref, all_keys_ref), (value_ref, all_values_ref)):
            target[0, : blocks * BLK] = source[...]
            total_ref[...] = jnp.zeros_like(total_ref)

            @pl.loop(0, blocks)
            def _(index):
                place = rows_of(section_ref[index])
                total_ref[place] += source[rows_of(index)].astype(jnp.float32)

            @pl.loop(0, sections)
            def _(index):
                target[0, rows_of(blocks + index)] = (
                    total_ref[rows_of(index)] / root_ref[index]
                ).astype(jnp.bfloat16)

    for g, part in enumerate(stacked(query_ref, heads)):
        stack_ref[g * BLK : (g + 1) * BLK] = part
    query = stack_ref[...]
    valid_count = count_ref[block]
    steps = (valid_count + GROUP - 1) // GROUP

    def gathered(source, step):
        return jnp.concatenate(
            [source[0, rows_of(order_ref[block, step * GROUP + w])] for w in range(GROUP)], axis=0
        )

    wide_ref[...] = jnp.full_like(wide_ref, neg_large)

    @pl.loop(0, steps)
    def _(step):
        scores = product(query, gathered(all_keys_ref, step), 1, 1)
        pieces = masked_scores(scores, step * GROUP, valid_count, heads)
        largest = wide_ref[...]
        for w, piece in enumerate(pieces):
            score_ref[step, :, w * BLK : (w + 1) * BLK] = piece
            largest = jnp.maximum(largest, piece)
        wide_ref[...] = largest

    largest = jnp.max(wide_ref[...], axis=1, keepdims=True) * to_base_two
    wide_ref[...] = jnp.zeros_like(wide_ref)

    @pl.loop(0, steps)
    def _(step):
        exponent = jnp.exp2(score_ref[step] * to_base_two - largest)
        score_ref[step] = exponent
        total = wide_ref[...]
        for w in range(GROUP):
            total = total + exponent[:, w * BLK : (w + 1) * BLK]
        wide_ref[...] = total

    total = jnp.sum(wide_ref[...], axis=1, keepdims=True)
    lse_ref[...] = jnp.broadcast_to(largest + jnp.log2(total), lse_ref.shape)
    inverse = 1.0 / total
    out_ref[...] = jnp.zeros_like(out_ref)

    @pl.loop(0, steps)
    def _(step):
        light = (score_ref[step] * inverse).astype(jnp.bfloat16)
        out_ref[...] += product(light, gathered(all_values_ref, step), 1, 0)

    for g in range(heads):
        attn_ref[:, g * HEAD_DIMENSION : (g + 1) * HEAD_DIMENSION] = out_ref[
            g * BLK : (g + 1) * BLK
        ].astype(jnp.bfloat16)


def backward_kernel(
    order_ref, count_ref, section_ref, rounded_ref, root_ref,
    query_ref, grad_ref, attn_ref, lse_ref, all_keys_ref, all_values_ref,
    grad_query_ref, terms_ref,
    query_stack, grad_stack, delta_ref, sum_ref, key_sum_ref, value_sum_ref,
):
    block = pl.program_id(1)
    last = pl.num_programs(1) - 1
    heads = query_ref.shape[1] // HEAD_DIMENSION
    blocks = terms_ref.shape[0] // BLK

    @pl.when(block == 0)
    def _():
        key_sum_ref[...] = jnp.zeros_like(key_sum_ref)
        value_sum_ref[...] = jnp.zeros_like(value_sum_ref)

    for g in range(heads):
        lanes = slice(g * HEAD_DIMENSION, (g + 1) * HEAD_DIMENSION)
        rows = slice(g * BLK, (g + 1) * BLK)
        query_stack[rows] = query_ref[:, lanes]
        grad = grad_ref[:, lanes]
        grad_stack[rows] = grad
        delta = jnp.sum(
            grad.astype(jnp.float32) * attn_ref[:, lanes].astype(jnp.float32), axis=1, keepdims=True
        )
        delta_ref[rows] = jnp.broadcast_to(delta, (BLK, BLK))
    query = query_stack[...]
    grad = grad_stack[...]
    valid_count = count_ref[block]
    steps = (valid_count + GROUP - 1) // GROUP
    sum_ref[...] = jnp.zeros_like(sum_ref)

    @pl.loop(0, steps)
    def _(step):
        places = [order_ref[block, step * GROUP + w] for w in range(GROUP)]
        keys = jnp.concatenate([all_keys_ref[0, rows_of(place)] for place in places], axis=0)
        values = jnp.concatenate([all_values_ref[0, rows_of(place)] for place in places], axis=0)
        scores = product(query, keys, 1, 1)
        d_weights = product(grad, values, 1, 1)
        lse = lse_ref[...]
        delta = delta_ref[...]
        light, d_scores = [], []
        for w, piece in enumerate(masked_scores(scores, step * GROUP, valid_count, heads)):
            weights = jnp.exp2(piece * to_base_two - lse)
            light.append(weights.astype(jnp.bfloat16))
            slope = d_weights[:, w * BLK : (w + 1) * BLK] - delta
            d_scores.append((weights * slope * scaling).astype(jnp.bfloat16))
        light = jnp.concatenate(light, axis=1)
        d_scores = jnp.concatenate(d_scores, axis=1)
        sum_ref[...] += product(d_scores, keys, 1, 0)
        key_terms = product(d_scores, query, 0, 0)
        value_terms = product(light, grad, 0, 0)
        for w, place in enumerate(places):
            rounds = rounded_ref[block, step * GROUP + w] > 0
            for terms, target in ((key_terms, key_sum_ref), (value_terms, value_sum_ref)):
                term = terms[w * BLK : (w + 1) * BLK]
                term = jnp.where(rounds, term.astype(jnp.bfloat16).astype(jnp.float32), term)
                target[rows_of(place)] += term

    for g in range(heads):
        grad_query_ref[:, g * HEAD_DIMENSION : (g + 1) * HEAD_DIMENSION] = sum_ref[
            g * BLK : (g + 1) * BLK
        ].astype(jnp.bfloat16)

    @pl.when(block == last)
    def _():
        @pl.loop(0, blocks)
        def _(index):
            section = section_ref[index]
            root = root_ref[section]
            for half, source in enumerate((key_sum_ref, value_sum_ref)):
                lanes = slice(half * HEAD_DIMENSION, (half + 1) * HEAD_DIMENSION)
                total = source[rows_of(index)] + source[rows_of(blocks + section)] / root
                terms_ref[rows_of(index), lanes] = total.astype(jnp.bfloat16)


def attention_forward(queries, pairs, order, count, block_section, root_counts):
    tokens, width = queries.shape
    kv_heads = pairs.shape[1] // (2 * HEAD_DIMENSION)
    heads = width // (kv_heads * HEAD_DIMENSION)
    blocks, sections = block_section.shape[0], root_counts.shape[0]
    own_blocks = tokens // BLK
    extended = (blocks + sections) * BLK
    rows = heads * BLK
    smem = pl.BlockSpec(memory_space=pltpu.SMEM)
    whole = pl.BlockSpec((1, extended, HEAD_DIMENSION), lambda c, b: (c, 0, 0))
    by_block = pl.BlockSpec((BLK, heads * HEAD_DIMENSION), lambda c, b: (b, c))
    matmul = 2 * tokens * SLOTS * BLK * width
    return pl.pallas_call(
        forward_kernel,
        name="attention_forward",
        grid=(kv_heads, own_blocks),
        in_specs=[
            smem, smem, smem, smem,
            by_block,
            pl.BlockSpec((blocks * BLK, HEAD_DIMENSION), lambda c, b: (0, 2 * c)),
            pl.BlockSpec((blocks * BLK, HEAD_DIMENSION), lambda c, b: (0, 2 * c + 1)),
        ],
        out_specs=[
            by_block,
            pl.BlockSpec((None, None, rows, HEAD_DIMENSION), lambda c, b: (c, b, 0, 0)),
            whole,
            whole,
        ],
        out_shape=[
            jax.ShapeDtypeStruct((tokens, width), jnp.bfloat16),
            jax.ShapeDtypeStruct((kv_heads, own_blocks, rows, HEAD_DIMENSION), jnp.float32),
            jax.ShapeDtypeStruct((kv_heads, extended, HEAD_DIMENSION), jnp.bfloat16),
            jax.ShapeDtypeStruct((kv_heads, extended, HEAD_DIMENSION), jnp.bfloat16),
        ],
        scratch_shapes=[
            pltpu.VMEM((rows, HEAD_DIMENSION), jnp.bfloat16),
            pltpu.VMEM((-(-SLOTS // GROUP), rows, GROUP * BLK), jnp.float32),
            pltpu.VMEM((rows, HEAD_DIMENSION), jnp.float32),
            pltpu.VMEM((rows, HEAD_DIMENSION), jnp.float32),
            pltpu.VMEM((sections * BLK, HEAD_DIMENSION), jnp.float32),
        ],
        compiler_params=pltpu.CompilerParams(vmem_limit_bytes=vmem_limit),
        cost_estimate=pl.CostEstimate(
            flops=2 * matmul, bytes_accessed=8 << 20, transcendentals=matmul // 256
        ),
    )(order, count, block_section, root_counts, queries, pairs, pairs)


def attention_backward(
    queries, d_attn, attn, lse, all_keys, all_values, order, count, rounded, block_section, root_counts
):
    tokens, width = queries.shape
    kv_heads, extended, _ = all_keys.shape
    heads = width // (kv_heads * HEAD_DIMENSION)
    blocks = block_section.shape[0]
    own_blocks = tokens // BLK
    rows = heads * BLK
    smem = pl.BlockSpec(memory_space=pltpu.SMEM)
    whole = pl.BlockSpec((1, extended, HEAD_DIMENSION), lambda c, b: (c, 0, 0))
    by_block = pl.BlockSpec((BLK, heads * HEAD_DIMENSION), lambda c, b: (b, c))
    matmul = 2 * tokens * SLOTS * BLK * width
    return pl.pallas_call(
        backward_kernel,
        name="attention_backward",
        grid=(kv_heads, own_blocks),
        in_specs=[
            smem, smem, smem, smem, smem,
            by_block, by_block, by_block,
            pl.BlockSpec((None, None, rows, HEAD_DIMENSION), lambda c, b: (c, b, 0, 0)),
            whole, whole,
        ],
        out_specs=[
            by_block,
            pl.BlockSpec((blocks * BLK, 2 * HEAD_DIMENSION), lambda c, b: (0, c)),
        ],
        out_shape=[
            jax.ShapeDtypeStruct((tokens, width), jnp.bfloat16),
            jax.ShapeDtypeStruct((blocks * BLK, kv_heads * 2 * HEAD_DIMENSION), jnp.bfloat16),
        ],
        scratch_shapes=[
            pltpu.VMEM((rows, HEAD_DIMENSION), jnp.bfloat16),
            pltpu.VMEM((rows, HEAD_DIMENSION), jnp.bfloat16),
            pltpu.VMEM((rows, HEAD_DIMENSION), jnp.float32),
            pltpu.VMEM((rows, HEAD_DIMENSION), jnp.float32),
            pltpu.VMEM((extended, HEAD_DIMENSION), jnp.float32),
            pltpu.VMEM((extended, HEAD_DIMENSION), jnp.float32),
        ],
        compiler_params=pltpu.CompilerParams(vmem_limit_bytes=vmem_limit),
        cost_estimate=pl.CostEstimate(
            flops=5 * matmul, bytes_accessed=16 << 20, transcendentals=matmul // 256
        ),
    )(
        order, count, block_section, rounded, root_counts,
        queries, d_attn, attn, lse, all_keys, all_values,
    )


def key_slots(block_section, section_parent, xref_owner, xref_block, xref_valid, first_blk):
    blocks = block_section.shape[0]
    blk_count = xref_block.shape[0]
    own = first_blk + jnp.arange(blk_count, dtype=jnp.int32)
    offsets = jnp.concatenate([jnp.array([0], jnp.int32), jnp.arange(1 - LOOK, 0, dtype=jnp.int32)])
    window = own[:, None] + offsets[None, :]
    is_block = jnp.arange(blocks, dtype=jnp.int32)

    def section_of(index):
        return jnp.sum(
            jnp.where(index[..., None] == is_block, block_section + 1, 0), axis=-1
        ) - 1

    my_sec = section_of(own)
    window_ok = section_of(window) == my_sec[:, None]
    chain = [my_sec]
    is_section = jnp.arange(section_parent.shape[0], dtype=jnp.int32)
    for _ in range(ANC - 1):
        prior = chain[-1]
        chain.append(
            jnp.sum(jnp.where(prior[:, None] == is_section, section_parent + 1, 0), axis=1) - 1
        )
    ancestors = jnp.stack(chain, axis=1)
    targets = xref_owner.reshape(blk_count, XREF) * blk_count + xref_block
    place = jnp.concatenate(
        [jnp.maximum(window, 0), blocks + jnp.maximum(ancestors, 0), targets], axis=1
    )
    valid = jnp.concatenate([window_ok, ancestors >= 0, xref_valid > 0], axis=1)
    slot = jnp.arange(SLOTS, dtype=jnp.int32)
    earlier = slot[:, None] < slot[None, :]
    before = jnp.sum(jnp.where(earlier[None], valid[:, :, None].astype(jnp.int32), 0), axis=1)
    count = jnp.sum(valid.astype(jnp.int32), axis=1)
    rank = jnp.where(valid, before, count[:, None] + slot - before)
    sorted_from = rank[:, :, None] == slot
    padded = -(-SLOTS // GROUP) * GROUP - SLOTS
    order = jnp.sum(jnp.where(sorted_from, place[:, :, None], 0), axis=1)
    is_ref = (slot >= LOOK + ANC).astype(jnp.int32)
    rounded = jnp.sum(jnp.where(sorted_from, is_ref[None, :, None], 0), axis=1)
    order, rounded = (jnp.pad(table, ((0, 0), (0, padded))) for table in (order, rounded))
    return order, rounded, count


def exchanged(block, axis, bit):
    size = lax.axis_size(axis)
    return lax.ppermute(block, axis, [(i, i ^ bit) for i in range(size)])


def gathered_by_exchange(block, axis):
    parts = block[None]
    bit = 1
    while bit < lax.axis_size(axis):
        parts = jnp.concatenate([parts, exchanged(parts, axis, bit)], axis=0)
        bit *= 2
    return parts


def cotangent_kernel(me_ref, left_ref, right_ref, out_ref, sum_ref):
    step = pl.program_id(0)

    @pl.when(step == 0)
    def _():
        sum_ref[...] = jnp.zeros_like(sum_ref)

    sum_ref[...] += product(left_ref[...], right_ref[...], 1, 0)

    @pl.when(step == pl.num_programs(0) - 1)
    def _():
        out_ref[...] = sum_ref[...].astype(jnp.bfloat16)


def cotangent_of_attn(parts, weight, me):
    count, tokens, part_width = parts.shape
    width = weight.shape[1]
    return pl.pallas_call(
        cotangent_kernel,
        name="cotangent_of_attn",
        grid_spec=pltpu.PrefetchScalarGridSpec(
            num_scalar_prefetch=1,
            grid=(count,),
            in_specs=[
                pl.BlockSpec((None, tokens, part_width), lambda j, me: (j, 0, 0)),
                pl.BlockSpec((part_width, width), lambda j, me: (me[0] ^ j, 0)),
            ],
            out_specs=pl.BlockSpec((tokens, width), lambda j, me: (0, 0)),
            scratch_shapes=[pltpu.VMEM((tokens, width), jnp.float32)],
        ),
        out_shape=jax.ShapeDtypeStruct((tokens, width), jnp.bfloat16),
        compiler_params=pltpu.CompilerParams(vmem_limit_bytes=vmem_limit),
        cost_estimate=pl.CostEstimate(
            flops=2 * count * tokens * part_width * width,
            bytes_accessed=2 * (parts.size + weight.size + tokens * width),
            transcendentals=0,
        ),
    )(me.reshape(1), parts, weight)


def projection_kernel(attn_ref, weight_ref, out_ref):
    out_ref[...] = product(attn_ref[...], weight_ref[...], 1, 1).astype(jnp.bfloat16)


def projection_parts(attn, weight, count):
    tokens, width = attn.shape
    part_width = weight.shape[0] // count
    return pl.pallas_call(
        projection_kernel,
        name="projection_parts",
        grid=(count,),
        in_specs=[
            pl.BlockSpec((tokens, width), lambda j: (0, 0)),
            pl.BlockSpec((part_width, width), lambda j: (j, 0)),
        ],
        out_specs=pl.BlockSpec((None, tokens, part_width), lambda j: (j, 0, 0)),
        out_shape=jax.ShapeDtypeStruct((count, tokens, part_width), jnp.bfloat16),
        compiler_params=pltpu.CompilerParams(vmem_limit_bytes=vmem_limit),
        cost_estimate=pl.CostEstimate(
            flops=2 * count * tokens * part_width * width,
            bytes_accessed=2 * (attn.size + weight.size + tokens * weight.shape[0]),
            transcendentals=0,
        ),
    )(attn, weight)


def on_device(
    queries,
    keys,
    values,
    out_weight,
    d_proj,
    block_section,
    section_parent,
    xref_owner,
    xref_block,
    xref_valid,
):
    tok_local = queries.shape[0]
    blk_count = tok_local // BLK
    kv_heads = keys.shape[1] // HEAD_DIMENSION
    head_count = lax.axis_size("head")
    first_blk = lax.axis_index("seq") * blk_count

    def columns(array, index):
        return array[:, index * HEAD_DIMENSION : (index + 1) * HEAD_DIMENSION]

    own_pairs = jnp.concatenate(
        [columns(array, c) for c in range(kv_heads) for array in (keys, values)], axis=1
    )
    pairs = lax.all_gather(own_pairs, "seq", axis=0, tiled=True)
    weight = lax.all_gather(out_weight.T, "seq", axis=0, tiled=True)
    d_parts = gathered_by_exchange(d_proj, "head")

    section_ids = jnp.arange(section_parent.shape[0], dtype=jnp.int32)
    root_counts = jnp.sqrt(
        jnp.sum((block_section[:, None] == section_ids[None, :]).astype(jnp.float32), axis=0)
    )
    order, rounded, count = key_slots(
        block_section, section_parent, xref_owner, xref_block, xref_valid, first_blk
    )
    attn, lse, all_keys, all_values = attention_forward(
        queries, pairs, order, count, block_section, root_counts
    )
    d_attn = cotangent_of_attn(d_parts, weight, lax.axis_index("head"))
    parts = projection_parts(attn, weight, head_count)
    projected = lax.psum_scatter(parts, "head", scatter_dimension=0, tiled=False)
    grad_queries, terms = attention_backward(
        queries, d_attn, attn, lse, all_keys, all_values,
        order, count, rounded, block_section, root_counts,
    )
    own_terms = lax.psum_scatter(terms, "seq", scatter_dimension=0, tiled=True)
    d_keys = jnp.concatenate([columns(own_terms, 2 * c) for c in range(kv_heads)], axis=1)
    d_values = jnp.concatenate([columns(own_terms, 2 * c + 1) for c in range(kv_heads)], axis=1)
    return (projected, grad_queries, d_keys, d_values)


def solution(mesh):
    placed = (
        P("seq", "head"),
        P("seq", "head"),
        P("seq", "head"),
        P("head", "seq"),
        P("seq", "head"),
        P(),
        P(),
        P("seq", None),
        P("seq", None),
        P("seq", None),
    )
    return jax.shard_map(
        on_device,
        mesh=mesh,
        in_specs=placed,
        out_specs=(P("seq", "head"), P("seq", "head"), P("seq", "head"), P("seq", "head")),
        check_vma=False,
    )
```

time: 927 us -> 384 us (0.41); the launches traced: 916 us -> 383 us
  local copies, waits for them, and re-layouts: 290 us -> 3.47 us
  matrix products: 224 us -> 0 us
  Pallas kernels: 0 us -> 101 us
  waiting for transfers between devices: 353 us -> 254 us
  starting transfers between devices: 26.1 us -> 3.59 us
    dot_general x36 -> x0, matrix products: 148 us -> none  [the longest x20 105 us: product(): return jnp.einsum(form, left, right, preferred_element_type=jnp.float32)]
    reduce_scatter x0 -> x2, waiting for transfers between devices: none -> 125 us  [the longest x1 90.4 us: on_device(): own_terms = lax.psum_scatter(terms, 'seq', scatter_dimension=0, tiled=True)]
    psum x2 -> x0, waiting for transfers between devices: 122 us -> none  [the longest x1 76.7 us: on_device(): lax.psum(section_dk.astype(jnp.bfloat16), 'seq').astype(jnp.float32)]
    pallas_call x0 -> x4, Pallas kernels: none -> 101 us  [the longest x1 43.6 us: attention_backward(): pl.pallas_call(backward_kernel, name='attention_backward', grid=(kv_heads...]
    all_to_all x3 -> x0, waiting for transfers between devices: 84.2 us -> none  [the longest x1 84.2 us: on_device(): lax.all_to_all(slot_dk, 'seq', split_axis=0, concat_axis=0, tiled=True)]
    sub x8 -> x0, matrix products: 75.9 us -> none  [softmax_weights(): exponent = jnp.where(allowed, jnp.exp(masked - row_max), 0.0)]
    while x13 -> x0, local copies, waits for them, and re-layouts: 46.2 us -> none  [the longest x2 28.7 us: on_device(): lax.map(run_backward, (query_blocks, key_sets, value_sets, allowed, attn_...]
    broadcast_in_dim x18 -> x0, local copies, waits for them, and re-layouts: 44.7 us -> none  [the longest x8 33.5 us: on_device(): lax.map(run_backward, (query_blocks, key_sets, value_sets, allowed, attn_...]
  transfers between devices with their start and end apart: 14 -> 6, of which waited for: 7 -> 6; matrix products, arithmetic and copies ran while one was open for 19% -> 2% of each run, Pallas kernels for 0% -> 13%
where the time goes in v1:
time: 384 us; the launch traced here: 383 us
  waiting for transfers between devices  254 us (66%)
  Pallas kernels  101 us (26%)
  between operations  13.9 us (4%)
  other arithmetic  7.57 us (2%)
    reduce_scatter x1, waiting for transfers between devices, on_device(): own_terms = lax.psum_scatter(terms, 'seq', scatter_dimension=0, tiled=True)  90.4 us
    all_gather x1, waiting for transfers between devices, on_device(): weight = lax.all_gather(out_weight.T, 'seq', axis=0, tiled=True)  62.1 us
    pallas_call x1, Pallas kernels, attention_backward(): pl.pallas_call(backward_kernel, name='attention_backward', grid=(kv_heads...  43.6 us
    pallas_call x1, Pallas kernels, attention_forward(): pl.pallas_call(forward_kernel, name='attention_forward', grid=(kv_heads,...  40.5 us
    all_gather x1, waiting for transfers between devices, on_device(): pairs = lax.all_gather(own_pairs, 'seq', axis=0, tiled=True)  38.7 us
    reduce_scatter x1, waiting for transfers between devices, on_device(): lax.psum_scatter(parts, 'head', scatter_dimension=0, tiled=False)  34.5 us
    ppermute x2, waiting for transfers between devices, exchanged(): return lax.ppermute(block, axis, [(i, i ^ bit) for i in range(size)])  27.6 us
    pallas_call x1, Pallas kernels, cotangent_of_attn(): pl.pallas_call(cotangent_kernel, name='cotangent_of_attn', grid_spec=pltp...  8.36 us
  transfers between devices with their start and end apart: 6, of which 6 were waited for; matrix products, arithmetic and copies ran while one was open for 2% of the time, Pallas kernels for 13%

profile of v1, /device:TPU:0, one launch (start us, length us, event | category | flops | bytes accessed | tf_op | source)
XLA Modules:
  0.0 383.2 jit_solution(6301274968731965940)
XLA Ops:
  7.3 1.2 fusion.2
  8.5 0.9 pad_maximum_fusion.2
  9.4 0.7 all-gather.5.cloned.1.call-update
  10.2 0.6 collective-permute-start
  10.8 0.2 select_reduce_fusion.5
  11.0 0.2 select_reduce_fusion.4
  11.3 0.1 copy.18
  11.4 0.2 select_reduce_fusion.3
  11.8 0.7 collective-permute-done
  12.4 1.2 pad_maximum_fusion.1
  13.6 2.9 collective-permute-start.1
  16.6 0.2 convert_reduce_fusion.1
  16.8 0.1 copy.19
  16.9 0.1 select_reduce_fusion.2
  17.1 0.1 copy.20
  17.4 0.1 copy.21
  17.5 0.1 convert_reduce_fusion
  17.7 0.5 sqrt.3.root_ref
  18.2 0.7 select_reduce_fusion
  18.9 26.9 %collective-permute-done.1 = bf16[2,512,640]{2,1,0:T(8,128)(2,1)S(1)} collective-permute-done((bf16[2,512,640]{2,1,0:T(8,128)(2,1)}, bf16[2,512,640]{2,1,0:T(8,128)(2,1)S(1)}, u32[]{:S(2)}, u32[]{:S(2)}) %collective-permute-start.1) | collective-permute-done | bytes 1310752 | tf_op jit(solution)/shard_map/ppermute | solution.py:350
  45.8 1.8 pad_maximum_fusion.left_ref
  47.6 38.7 %all-gather.3.cloned.1.call-done.key_ref.value_ref = bf16[4096,512]{1,0:T(8,128)(2,1)} async-done(((bf16[512,512]{1,0:T(8,128)(2,1)}), bf16[4096,512]{1,0:T(8,128)(2,1)}) %all-gather.3.cloned.1.call-update) | async-done | bytes 4194320 | tf_op jit(solution)/shard_map/all_gather | solution.py:452
  86.3 40.5 %attention_forward.1 = (bf16[512,1280]{1,0:T(8,128)(2,1)}, f32[2,4,640,128]{3,2,1,0:T(8,128)}, bf16[2,4608,128]{2,1,0:T(8,128)(2,1)}, bf16[2,4608,128]{2,1,0:T(8,128)(2,1)}) custom-call(s32[4,18]{1,0:T(4,128)} %get-tuple-element.17.order_ref, s32[4]{0:T(128)} %copy-done.2, s32[32]{0:T(128)} %section_ref.3, f32[4]{0:T(128)} %sqrt.3.root_ref, ...), custom_call_target="tpu_custom_call" | custom-call | flops 6039797760 | bytes 8388608 | tf_op jit(solution)/shard_map/attention_forward/pallas_call | solution.py:221
  126.8 62.1 %all-gather.5.cloned.1.call-done.weight_ref.right_ref = bf16[2560,1280]{1,0:T(8,128)(2,1)} async-done(((bf16[320,1280]{1,0:T(8,128)(2,1)}), bf16[2560,1280]{1,0:T(8,128)(2,1)}) %all-gather.5.cloned.1.call-update) | async-done | bytes 6553616 | tf_op jit(solution)/shard_map/all_gather | solution.py:453
  188.9 8.4 %cotangent_of_attn.1.grad_ref = bf16[512,1280]{1,0:T(8,128)(2,1)} custom-call(s32[1]{0:T(128)} %bitcast.4.me_ref, bf16[4,512,640]{2,1,0:T(8,128)(2,1)} %pad_maximum_fusion.left_ref, bf16[2560,1280]{1,0:T(8,128)(2,1)} %all-gather.5.cloned.1.call-done.weight_ref.right_ref), custom_call_target="tpu_custom_call" | custom-call | flops 3355443200 | bytes 10485760 | tf_op jit(solution)/shard_map/cotangent_of_attn/pallas_call | solution.py:379
  197.3 43.6 %attention_backward.1 = (bf16[512,1280]{1,0:T(8,128)(2,1)}, bf16[4096,512]{1,0:T(8,128)(2,1)}) custom-call(s32[4,18]{1,0:T(4,128)} %get-tuple-element.17.order_ref, s32[4]{0:T(128)} %copy-done.2, s32[32]{0:T(128)} %section_ref.3, s32[4,18]{1,0:T(4,128)} %get-tuple-element.16.rounded_ref, f32[4]{0:T(128)} %sqrt.3.root_ref, bf16[512,1280]{1,0:T(8,128)(2,1)} %query_ref.3, ...), custom_call_target="tpu_custom_call" | custom-call | flops 15099494400 | bytes 16777216 | tf_op jit(solution)/shard_map/attention_backward/pallas_call | solution.py:270
  241.0 8.2 %projection_parts.1 = bf16[4,512,640]{2,1,0:T(8,128)(2,1)} custom-call(bf16[512,1280]{1,0:T(8,128)(2,1)} %get-tuple-element.10.attn_ref, bf16[2560,1280]{1,0:T(8,128)(2,1)} %all-gather.5.cloned.1.call-done.weight_ref.right_ref), custom_call_target="tpu_custom_call" | custom-call | flops 3355443200 | bytes 10485760 | tf_op jit(solution)/shard_map/projection_parts/pallas_call | solution.py:409
  249.1 90.4 %reduce-scatter.5.cloned.1.call-done = bf16[512,512]{1,0:T(8,128)(2,1)} async-done(((bf16[4096,512]{1,0:T(8,128)(2,1)}), bf16[512,512]{1,0:T(8,128)(2,1)}) %reduce-scatter.5.cloned.1.call-update) | async-done | bytes 524304 | tf_op jit(solution)/shard_map/reduce_scatter | solution.py:473
  339.5 1.1 fusion.1
  340.6 0.7 pad_maximum_fusion.3
  341.4 0.7 pad_maximum_fusion.4
  342.1 34.5 %reduce-scatter.3.cloned.1.call-done = bf16[1,512,640]{2,1,0:T(8,128)(2,1)} async-done(((bf16[4,512,640]{2,1,0:T(8,128)(2,1)}), bf16[1,512,640]{2,1,0:T(8,128)(2,1)}) %reduce-scatter.3.cloned.1.call-update) | async-done | bytes 655376 | tf_op jit(solution)/shard_map/reduce_scatter | solution.py:468
  (41 shorter events, 1.0 us)
Async XLA Ops:
  7.2 3.0 copy-start
  7.2 3.6 copy-start.6
  7.2 3.8 copy-start.4
  7.2 4.5 %copy-start.3 = (s32[4,12]{1,0:T(4,128)S(1)}, s32[4,12]{1,0:T(4,128)}, u32[]{:S(2)}) copy-start(s32[4,12]{1,0:T(4,128)} %param.20) | copy-start | bytes 580
  7.2 79.1 %all-gather.3.cloned.1.call-start = ((), (), s32[]{:S(2)}) async-start(), calls=%async_computation.2 | async-start | bytes 4718592 | tf_op jit(solution)/shard_map/all_gather | solution.py:452
  8.4 8.7 %copy-start.5 = (s32[48,1]{0,1:T(1,128)S(1)}, s32[48,1]{0,1:T(1,128)}, u32[]{:S(2)}) copy-start(s32[48,1]{0,1:T(1,128)} %param.18) | copy-start | bytes 580
  8.5 8.8 %copy-start.1 = (s32[4,12]{1,0:T(4,128)S(1)}, s32[4,12]{1,0:T(4,128)}, u32[]{:S(2)}) copy-start(s32[4,12]{1,0:T(4,128)} %param.19) | copy-start | bytes 580
  9.3 179.6 %all-gather.5.cloned.1.call-start = ((), (), s32[]{:S(2)}) async-start(), calls=%async_computation.3 | async-start | bytes 7372800 | tf_op jit(solution)/shard_map/all_gather | solution.py:453
  10.1 329.4 %reduce-scatter.5.cloned.1.call-start = ((), (), s32[]{:S(2)}) async-start(), calls=%async_computation.5 | async-start | bytes 4718592 | tf_op jit(solution)/shard_map/reduce_scatter | solution.py:473
  10.2 2.3 collective-permute-start
  13.6 32.2 %collective-permute-start.1 = (bf16[2,512,640]{2,1,0:T(8,128)(2,1)}, bf16[2,512,640]{2,1,0:T(8,128)(2,1)S(1)}, u32[]{:S(2)}, u32[]{:S(2)}) collective-permute-start(bf16[2,512,640]{2,1,0:T(8,128)(2,1)} %pad_maximum_fusion.1), channel_id=1, source_target_pairs={{0,2},{1,3},{2,0},{3,1},{4,6},{5,7},{6,4},{7,5},{8,10},{9,11},{10,... | collective-permute-start | bytes 3932168 | tf_op jit(solution)/shard_map/ppermute | solution.py:350
  16.8 30.8 %copy-start.2 = (s32[4]{0:T(128)}, s32[4]{0:T(128)S(1)}, u32[]{:S(2)}) copy-start(s32[4]{0:T(128)S(1)} %get-tuple-element.18.count_ref) | copy-start | bytes 52
  240.9 135.7 %reduce-scatter.3.cloned.1.call-start = ((), (), s32[]{:S(2)}) async-start(), calls=%async_computation.4 | async-start | bytes 3276800 | tf_op jit(solution)/shard_map/reduce_scatter | solution.py:468
Sparse Core Ops, SparseCore 0:
  10.7 75.4 all-gather.2
  88.4 100.4 all-gather.4
  241.0 98.4 reduce-scatter.4
  342.5 34.1 reduce-scatter.2

commit v2 on v1

--- a/solution.py
+++ b/solution.py
@@ -51,31 +51,33 @@
     return pieces
 
 
-def forward_kernel(
-    order_ref, count_ref, section_ref, root_ref,
-    query_ref, key_ref, value_ref,
-    attn_ref, lse_ref, all_keys_ref, all_values_ref,
-    stack_ref, score_ref, wide_ref, out_ref, total_ref,
-):
-    block = pl.program_id(1)
+def forward_kernel(shard_rows, *refs):
+    order_ref, count_ref, section_ref, root_ref, place_ref, query_ref = refs[:6]
+    shard_refs = refs[6 : 6 + len(shard_rows)]
+    (attn_ref, lse_ref, all_keys_ref, all_values_ref,
+     stack_ref, score_ref, wide_ref, out_ref, total_ref) = refs[6 + len(shard_rows) :]
+    block = pl.program_id(0)
     heads = query_ref.shape[1] // HEAD_DIMENSION
-    blocks = key_ref.shape[0] // BLK
+    blocks = section_ref.shape[0]
     sections = root_ref.shape[0]
 
     @pl.when(block == 0)
     def _():
-        for source, target in ((key_ref, all_keys_ref), (value_ref, all_values_ref)):
-            target[0, : blocks * BLK] = source[...]
+        for half, target in enumerate((all_keys_ref, all_values_ref)):
+            lanes = slice(half * HEAD_DIMENSION, (half + 1) * HEAD_DIMENSION)
+            for number, (shard_ref, rows) in enumerate(zip(shard_refs, shard_rows)):
+                first = pl.multiple_of(place_ref[number], BLK)
+                target[pl.ds(first, rows)] = shard_ref[:, lanes]
             total_ref[...] = jnp.zeros_like(total_ref)
 
             @pl.loop(0, blocks)
             def _(index):
                 place = rows_of(section_ref[index])
-                total_ref[place] += source[rows_of(index)].astype(jnp.float32)
+                total_ref[place] += target[rows_of(index)].astype(jnp.float32)
 
             @pl.loop(0, sections)
             def _(index):
-                target[0, rows_of(blocks + index)] = (
+                target[rows_of(blocks + index)] = (
                     total_ref[rows_of(index)] / root_ref[index]
                 ).astype(jnp.bfloat16)
 
@@ -87,7 +89,7 @@
 
     def gathered(source, step):
         return jnp.concatenate(
-            [source[0, rows_of(order_ref[block, step * GROUP + w])] for w in range(GROUP)], axis=0
+            [source[rows_of(order_ref[block, step * GROUP + w])] for w in range(GROUP)], axis=0
         )
 
     wide_ref[...] = jnp.full_like(wide_ref, neg_large)
@@ -136,8 +138,8 @@
     grad_query_ref, terms_ref,
     query_stack, grad_stack, delta_ref, sum_ref, key_sum_ref, value_sum_ref,
 ):
-    block = pl.program_id(1)
-    last = pl.num_programs(1) - 1
+    block = pl.program_id(0)
+    last = pl.num_programs(0) - 1
     heads = query_ref.shape[1] // HEAD_DIMENSION
     blocks = terms_ref.shape[0] // BLK
 
@@ -165,8 +167,8 @@
     @pl.loop(0, steps)
     def _(step):
         places = [order_ref[block, step * GROUP + w] for w in range(GROUP)]
-        keys = jnp.concatenate([all_keys_ref[0, rows_of(place)] for place in places], axis=0)
-        values = jnp.concatenate([all_values_ref[0, rows_of(place)] for place in places], axis=0)
+        keys = jnp.concatenate([all_keys_ref[rows_of(place)] for place in places], axis=0)
+        values = jnp.concatenate([all_values_ref[rows_of(place)] for place in places], axis=0)
         scores = product(query, keys, 1, 1)
         d_weights = product(grad, values, 1, 1)
         lse = lse_ref[...]
@@ -206,39 +208,36 @@
                 terms_ref[rows_of(index), lanes] = total.astype(jnp.bfloat16)
 
 
-def attention_forward(queries, pairs, order, count, block_section, root_counts):
-    tokens, width = queries.shape
-    kv_heads = pairs.shape[1] // (2 * HEAD_DIMENSION)
-    heads = width // (kv_heads * HEAD_DIMENSION)
+def attention_forward(queries, head, kv_heads, shards, places, order, count, block_section, root_counts):
+    tokens = queries.shape[0]
+    width = queries.shape[1] // kv_heads
     blocks, sections = block_section.shape[0], root_counts.shape[0]
     own_blocks = tokens // BLK
     extended = (blocks + sections) * BLK
-    rows = heads * BLK
+    rows = width // HEAD_DIMENSION * BLK
     smem = pl.BlockSpec(memory_space=pltpu.SMEM)
-    whole = pl.BlockSpec((1, extended, HEAD_DIMENSION), lambda c, b: (c, 0, 0))
-    by_block = pl.BlockSpec((BLK, heads * HEAD_DIMENSION), lambda c, b: (b, c))
+    whole = pl.BlockSpec((extended, HEAD_DIMENSION), lambda b: (0, 0))
     matmul = 2 * tokens * SLOTS * BLK * width
     return pl.pallas_call(
-        forward_kernel,
+        functools.partial(forward_kernel, [shard.shape[0] for shard in shards]),
         name="attention_forward",
-        grid=(kv_heads, own_blocks),
+        grid=(own_blocks,),
         in_specs=[
-            smem, smem, smem, smem,
-            by_block,
-            pl.BlockSpec((blocks * BLK, HEAD_DIMENSION), lambda c, b: (0, 2 * c)),
-            pl.BlockSpec((blocks * BLK, HEAD_DIMENSION), lambda c, b: (0, 2 * c + 1)),
+            smem, smem, smem, smem, smem,
+            pl.BlockSpec((BLK, width), lambda b: (b, head)),
+            *[pl.BlockSpec(shard.shape, lambda b: (0, 0)) for shard in shards],
         ],
         out_specs=[
-            by_block,
-            pl.BlockSpec((None, None, rows, HEAD_DIMENSION), lambda c, b: (c, b, 0, 0)),
+            pl.BlockSpec((BLK, width), lambda b: (b, 0)),
+            pl.BlockSpec((None, rows, HEAD_DIMENSION), lambda b: (b, 0, 0)),
             whole,
             whole,
         ],
         out_shape=[
             jax.ShapeDtypeStruct((tokens, width), jnp.bfloat16),
-            jax.ShapeDtypeStruct((kv_heads, own_blocks, rows, HEAD_DIMENSION), jnp.float32),
-            jax.ShapeDtypeStruct((kv_heads, extended, HEAD_DIMENSION), jnp.bfloat16),
-            jax.ShapeDtypeStruct((kv_heads, extended, HEAD_DIMENSION), jnp.bfloat16),
+            jax.ShapeDtypeStruct((own_blocks, rows, HEAD_DIMENSION), jnp.float32),
+            jax.ShapeDtypeStruct((extended, HEAD_DIMENSION), jnp.bfloat16),
+            jax.ShapeDtypeStruct((extended, HEAD_DIMENSION), jnp.bfloat16),
         ],
         scratch_shapes=[
             pltpu.VMEM((rows, HEAD_DIMENSION), jnp.bfloat16),
@@ -251,39 +250,40 @@
         cost_estimate=pl.CostEstimate(
             flops=2 * matmul, bytes_accessed=8 << 20, transcendentals=matmul // 256
         ),
-    )(order, count, block_section, root_counts, queries, pairs, pairs)
+    )(order, count, block_section, root_counts, places, queries, *shards)
 
 
 def attention_backward(
-    queries, d_attn, attn, lse, all_keys, all_values, order, count, rounded, block_section, root_counts
+    queries, head, d_attn, attn, lse, all_keys, all_values, order, count, rounded, block_section, root_counts
 ):
-    tokens, width = queries.shape
-    kv_heads, extended, _ = all_keys.shape
-    heads = width // (kv_heads * HEAD_DIMENSION)
+    tokens, width = attn.shape
+    extended, _ = all_keys.shape
     blocks = block_section.shape[0]
     own_blocks = tokens // BLK
-    rows = heads * BLK
+    rows = width // HEAD_DIMENSION * BLK
     smem = pl.BlockSpec(memory_space=pltpu.SMEM)
-    whole = pl.BlockSpec((1, extended, HEAD_DIMENSION), lambda c, b: (c, 0, 0))
-    by_block = pl.BlockSpec((BLK, heads * HEAD_DIMENSION), lambda c, b: (b, c))
+    whole = pl.BlockSpec((extended, HEAD_DIMENSION), lambda b: (0, 0))
+    by_block = pl.BlockSpec((BLK, width), lambda b: (b, 0))
     matmul = 2 * tokens * SLOTS * BLK * width
     return pl.pallas_call(
         backward_kernel,
         name="attention_backward",
-        grid=(kv_heads, own_blocks),
+        grid=(own_blocks,),
         in_specs=[
             smem, smem, smem, smem, smem,
-            by_block, by_block, by_block,
-            pl.BlockSpec((None, None, rows, HEAD_DIMENSION), lambda c, b: (c, b, 0, 0)),
+            pl.BlockSpec((BLK, width), lambda b: (b, head)),
+            pl.BlockSpec((BLK, width), lambda b: (b, head)),
+            by_block,
+            pl.BlockSpec((None, rows, HEAD_DIMENSION), lambda b: (b, 0, 0)),
             whole, whole,
         ],
         out_specs=[
             by_block,
-            pl.BlockSpec((blocks * BLK, 2 * HEAD_DIMENSION), lambda c, b: (0, c)),
+            pl.BlockSpec((blocks * BLK, 2 * HEAD_DIMENSION), lambda b: (0, 0)),
         ],
         out_shape=[
             jax.ShapeDtypeStruct((tokens, width), jnp.bfloat16),
-            jax.ShapeDtypeStruct((blocks * BLK, kv_heads * 2 * HEAD_DIMENSION), jnp.bfloat16),
+            jax.ShapeDtypeStruct((blocks * BLK, 2 * HEAD_DIMENSION), jnp.bfloat16),
         ],
         scratch_shapes=[
             pltpu.VMEM((rows, HEAD_DIMENSION), jnp.bfloat16),
@@ -301,6 +301,59 @@
         order, count, block_section, rounded, root_counts,
         queries, d_attn, attn, lse, all_keys, all_values,
     )
+
+
+class Ring:
+    def __init__(self, axis):
+        self.axis = axis
+        self.size = size = lax.axis_size(axis)
+        self.cycle = [*range(0, size, 2), *reversed(range(1, size, 2))]
+        at = [self.cycle.index(i) for i in range(size)]
+        self.position = jnp.array(at, jnp.int32)[lax.axis_index(axis)]
+        self.table = jnp.array(self.cycle, jnp.int32)
+
+    def index_at(self, distance):
+        return self.table[(self.position + distance) % self.size]
+
+    def sent(self, block, direction):
+        cycle, size = self.cycle, self.size
+        route = [(cycle[k], cycle[(k + direction) % size]) for k in range(size)]
+        return lax.ppermute(block, self.axis, route)
+
+    def gathered(self, block):
+        rows, half = block.shape[0], block.shape[0] // 2
+        pieces, firsts = [block], [self.index_at(0) * rows]
+        ahead, back = block, block
+        for step in range(1, self.size // 2):
+            ahead, back = self.sent(ahead, 1), self.sent(back, -1)
+            pieces += [ahead, back]
+            firsts += [self.index_at(-step) * rows, self.index_at(step) * rows]
+        far = self.index_at(self.size // 2) * rows
+        pieces += [self.sent(ahead[:half], 1), self.sent(back[half:], -1)]
+        firsts += [far, far + half]
+        return pieces, jnp.stack(firsts)
+
+    def reduced(self, terms):
+        rows = terms.shape[0] // self.size
+        half = rows // 2
+
+        def chunk(distance):
+            return lax.dynamic_slice_in_dim(terms, self.index_at(distance) * rows, rows)
+
+        def added(*arrays):
+            return sum(array.astype(jnp.float32) for array in arrays).astype(jnp.bfloat16)
+
+        far = chunk(self.size // 2)
+        ahead, back = self.sent(far[:half], 1), self.sent(far[half:], -1)
+        for step in range(self.size // 2 - 1, 0, -1):
+            up, down = chunk(step), chunk(-step)
+            if step == self.size // 2 - 1:
+                ahead = jnp.concatenate([added(up[:half], ahead), up[half:]])
+                back = jnp.concatenate([down[:half], added(down[half:], back)])
+            else:
+                ahead, back = added(up, ahead), added(down, back)
+            ahead, back = self.sent(ahead, 1), self.sent(back, -1)
+        return added(chunk(0), ahead, back)
 
 
 def key_slots(block_section, section_parent, xref_owner, xref_block, xref_valid, first_blk):
@@ -357,6 +410,15 @@
         parts = jnp.concatenate([parts, exchanged(parts, axis, bit)], axis=0)
         bit *= 2
     return parts
+
+
+def reduced_by_exchange(parts, axis):
+    bit = lax.axis_size(axis) // 2
+    while bit:
+        kept, given = parts[:bit], exchanged(parts[bit:], axis, bit)
+        parts = (kept.astype(jnp.float32) + given.astype(jnp.float32)).astype(jnp.bfloat16)
+        bit //= 2
+    return parts[0]
 
 
 def cotangent_kernel(me_ref, left_ref, right_ref, out_ref, sum_ref):
@@ -399,22 +461,25 @@
     )(me.reshape(1), parts, weight)
 
 
-def projection_kernel(attn_ref, weight_ref, out_ref):
+def projection_kernel(me_ref, attn_ref, weight_ref, out_ref):
     out_ref[...] = product(attn_ref[...], weight_ref[...], 1, 1).astype(jnp.bfloat16)
 
 
-def projection_parts(attn, weight, count):
+def projection_parts(attn, weight, count, me):
     tokens, width = attn.shape
     part_width = weight.shape[0] // count
     return pl.pallas_call(
         projection_kernel,
         name="projection_parts",
-        grid=(count,),
-        in_specs=[
-            pl.BlockSpec((tokens, width), lambda j: (0, 0)),
-            pl.BlockSpec((part_width, width), lambda j: (j, 0)),
-        ],
-        out_specs=pl.BlockSpec((None, tokens, part_width), lambda j: (j, 0, 0)),
+        grid_spec=pltpu.PrefetchScalarGridSpec(
+            num_scalar_prefetch=1,
+            grid=(count,),
+            in_specs=[
+                pl.BlockSpec((tokens, width), lambda j, me: (0, 0)),
+                pl.BlockSpec((part_width, width), lambda j, me: (me[0] ^ j, 0)),
+            ],
+            out_specs=pl.BlockSpec((None, tokens, part_width), lambda j, me: (j, 0, 0)),
+        ),
         out_shape=jax.ShapeDtypeStruct((count, tokens, part_width), jnp.bfloat16),
         compiler_params=pltpu.CompilerParams(vmem_limit_bytes=vmem_limit),
         cost_estimate=pl.CostEstimate(
@@ -422,7 +487,7 @@
             bytes_accessed=2 * (attn.size + weight.size + tokens * weight.shape[0]),
             transcendentals=0,
         ),
-    )(attn, weight)
+    )(me.reshape(1), attn, weight)
 
 
 def on_device(
@@ -446,10 +511,11 @@
     def columns(array, index):
         return array[:, index * HEAD_DIMENSION : (index + 1) * HEAD_DIMENSION]
 
-    own_pairs = jnp.concatenate(
-        [columns(array, c) for c in range(kv_heads) for array in (keys, values)], axis=1
-    )
-    pairs = lax.all_gather(own_pairs, "seq", axis=0, tiled=True)
+    ring = Ring("seq")
+    gathers = [
+        ring.gathered(jnp.concatenate([columns(keys, c), columns(values, c)], axis=1))
+        for c in range(kv_heads)
+    ]
     weight = lax.all_gather(out_weight.T, "seq", axis=0, tiled=True)
     d_parts = gathered_by_exchange(d_proj, "head")
 
@@ -460,20 +526,28 @@
     order, rounded, count = key_slots(
         block_section, section_parent, xref_owner, xref_block, xref_valid, first_blk
     )
-    attn, lse, all_keys, all_values = attention_forward(
-        queries, pairs, order, count, block_section, root_counts
-    )
+    tables = (block_section, root_counts)
+    forward = [
+        attention_forward(queries, c, kv_heads, *gathers[c], order, count, *tables)
+        for c in range(kv_heads)
+    ]
     d_attn = cotangent_of_attn(d_parts, weight, lax.axis_index("head"))
-    parts = projection_parts(attn, weight, head_count)
-    projected = lax.psum_scatter(parts, "head", scatter_dimension=0, tiled=False)
-    grad_queries, terms = attention_backward(
-        queries, d_attn, attn, lse, all_keys, all_values,
-        order, count, rounded, block_section, root_counts,
-    )
-    own_terms = lax.psum_scatter(terms, "seq", scatter_dimension=0, tiled=True)
-    d_keys = jnp.concatenate([columns(own_terms, 2 * c) for c in range(kv_heads)], axis=1)
-    d_values = jnp.concatenate([columns(own_terms, 2 * c + 1) for c in range(kv_heads)], axis=1)
-    return (projected, grad_queries, d_keys, d_values)
+    attn = jnp.concatenate([forward[c][0] for c in range(kv_heads)], axis=1)
+    parts = projection_parts(attn, weight, head_count, lax.axis_index("head"))
+    projected = reduced_by_exchange(parts, "head")
+    grad_queries, grad_keys, grad_values = [], [], []
+    for c in range(kv_heads):
+        grad_query, terms = attention_backward(
+            queries, c, d_attn, *forward[c], order, count, rounded, *tables
+        )
+        own_terms = ring.reduced(terms)
+        grad_queries.append(grad_query)
+        grad_keys.append(columns(own_terms, 0))
+        grad_values.append(columns(own_terms, 1))
+    d_queries, d_keys, d_values = (
+        jnp.concatenate(arrays, axis=1) for arrays in (grad_queries, grad_keys, grad_values)
+    )
+    return (projected, d_queries, d_keys, d_values)
 
 
 def solution(mesh):

time: 384 us -> 283 us (0.74)
  waiting for transfers between devices: 254 us -> 45.8 us
  starting transfers between devices: 3.59 us -> 56.4 us
  other arithmetic: 7.57 us -> 29.9 us
  Pallas kernels: 101 us -> 115 us
  between operations: 13.9 us -> 25.2 us
  local copies, waits for them, and re-layouts: 3.47 us -> 10.4 us
    reduce_scatter x2 -> x0, waiting for transfers between devices: 125 us -> none  [the longest x1 90.4 us: on_device(): own_terms = lax.psum_scatter(terms, 'seq', scatter_dimension=0, tiled=True)]
    all_gather x1, waiting for transfers between devices: 62.1 us -> 1.9 us  [on_device(): weight = lax.all_gather(out_weight.T, 'seq', axis=0, tiled=True)]
    ppermute x0 -> x32, starting transfers between devices: none -> 53 us  [sent(): return lax.ppermute(block, self.axis, route)]
    ppermute x0 -> x32, waiting for transfers between devices: none -> 42.7 us  [sent(): return lax.ppermute(block, self.axis, route)]
    all_gather x1 -> x0, waiting for transfers between devices: 38.7 us -> none  [on_device(): pairs = lax.all_gather(own_pairs, 'seq', axis=0, tiled=True)]
    ppermute x2 -> x4, waiting for transfers between devices: 27.6 us -> 0.57 us  [exchanged(): return lax.ppermute(block, axis, [(i, i ^ bit) for i in range(size)])]
    pallas_call x3 -> x5, Pallas kernels: 92.3 us -> 107 us  [the longest x2 51.1 us: attention_backward(): pl.pallas_call(backward_kernel, name='attention_backward', grid=(own_bloc...]
    convert_element_type x0 -> x11, other arithmetic: none -> 14.5 us  [the longest x10 12.8 us: added(): sum((array.astype(jnp.float32) for array in arrays)).astype(jnp.bfloat16)]
  transfers between devices with their start and end apart: 6 -> 37, of which waited for: 6 -> 14; matrix products, arithmetic and copies ran while one was open for 2% -> 13% of each run, Pallas kernels for 13% -> 29%
where the time goes in v2:
time: 283 us
  Pallas kernels  115 us (41%)
  starting transfers between devices  56.4 us (20%)
  waiting for transfers between devices  45.8 us (16%)
  other arithmetic  29.9 us (11%)
  between operations  25.2 us (9%)
  local copies, waits for them, and re-layouts  10.4 us (4%)
    ppermute x32, starting transfers between devices, sent(): return lax.ppermute(block, self.axis, route)  53 us
    pallas_call x2, Pallas kernels, attention_backward(): pl.pallas_call(backward_kernel, name='attention_backward', grid=(own_bloc...  51.1 us
    pallas_call x2, Pallas kernels, attention_forward(): pl.pallas_call(functools.partial(forward_kernel, [shard.shape[0] for shar...  47.7 us
    ppermute x32, waiting for transfers between devices, sent(): return lax.ppermute(block, self.axis, route)  42.7 us
    convert_element_type x10, other arithmetic, added(): sum((array.astype(jnp.float32) for array in arrays)).astype(jnp.bfloat16)  12.8 us
    pallas_call x1, Pallas kernels, cotangent_of_attn(): pl.pallas_call(cotangent_kernel, name='cotangent_of_attn', grid_spec=pltp...  8.35 us
    pallas_call x1, Pallas kernels, projection_parts(): pl.pallas_call(projection_kernel, name='projection_parts', grid_spec=pltp...  8.11 us
  transfers between devices with their start and end apart: 37, of which 14 were waited for; matrix products, arithmetic and copies ran while one was open for 13% of the time, Pallas kernels for 29%

profile of v2, /device:TPU:0, one launch (start us, length us, event | category | flops | bytes accessed | tf_op | source)
XLA Modules:
  0.0 283.0 jit_solution(2901292589683389692)
XLA Ops:
  9.2 3.1 %collective-permute-start = (bf16[512,256]{1,0:T(8,128)(2,1)S(1)}, bf16[512,256]{1,0:T(8,128)(2,1)S(1)}, u32[]{:S(2)}, u32[]{:S(2)}) collective-permute-start(bf16[512,256]{1,0:T(8,128)(2,1)S(1)} %pad_maximum_fusion.4.refs_6_), channel_id=1, source_target_pairs={{0,8},{8,16},{16,24},{24,28},{28,20},{20,12},{12,4},{4,0},{1,9},{9... | collective-permute-start | bytes 786440 | tf_op jit(solution)/shard_map/ppermute | solution.py:321
  12.3 2.1 collective-permute-start.8
  15.9 3.4 %collective-permute-done.refs_7_ = bf16[512,256]{1,0:T(8,128)(2,1)S(1)} collective-permute-done((bf16[512,256]{1,0:T(8,128)(2,1)S(1)}, bf16[512,256]{1,0:T(8,128)(2,1)S(1)}, u32[]{:S(2)}, u32[]{:S(2)}) %collective-permute-start) | collective-permute-done | bytes 262176 | tf_op jit(solution)/shard_map/ppermute | solution.py:321
  19.4 2.1 collective-permute-start.2
  21.6 5.5 %collective-permute-done.8.refs_7_ = bf16[512,256]{1,0:T(8,128)(2,1)S(1)} collective-permute-done((bf16[512,256]{1,0:T(8,128)(2,1)S(1)}, bf16[512,256]{1,0:T(8,128)(2,1)S(1)}, u32[]{:S(2)}, u32[]{:S(2)}) %collective-permute-start.8) | collective-permute-done | bytes 262176 | tf_op jit(solution)/shard_map/ppermute | solution.py:321
  27.0 2.8 %collective-permute-start.10 = (bf16[512,256]{1,0:T(8,128)(2,1)S(1)}, bf16[512,256]{1,0:T(8,128)(2,1)}, u32[]{:S(2)}, u32[]{:S(2)}) collective-permute-start(bf16[512,256]{1,0:T(8,128)(2,1)S(1)} %collective-permute-done.8.refs_7_), channel_id=1, source_target_pairs={{0,8},{8,16},{16,24},{24,28},{28,20},{20,12},{12,4},{4,0},{1,9},{9... | collective-permute-start | bytes 786440 | tf_op jit(solution)/shard_map/ppermute | solution.py:321
  29.9 2.4 collective-permute-done.9.refs_8_
  32.4 5.8 %collective-permute-done.2.refs_9_ = bf16[512,256]{1,0:T(8,128)(2,1)} collective-permute-done((bf16[512,256]{1,0:T(8,128)(2,1)S(1)}, bf16[512,256]{1,0:T(8,128)(2,1)}, u32[]{:S(2)}, u32[]{:S(2)}) %collective-permute-start.2) | collective-permute-done | bytes 262176 | tf_op jit(solution)/shard_map/ppermute | solution.py:321
  38.3 6.9 %collective-permute-start.4 = (bf16[512,256]{1,0:T(8,128)(2,1)}, bf16[512,256]{1,0:T(8,128)(2,1)S(1)}, u32[]{:S(2)}, u32[]{:S(2)}) collective-permute-start(bf16[512,256]{1,0:T(8,128)(2,1)} %collective-permute-done.2.refs_9_), channel_id=1, source_target_pairs={{0,8},{8,16},{16,24},{24,28},{28,20},{20,12},{12,4},{4,0},{1,9},{9... | collective-permute-start | bytes 786440 | tf_op jit(solution)/shard_map/ppermute | solution.py:321
  45.2 4.7 %collective-permute-done.3.refs_10_ = bf16[512,256]{1,0:T(8,128)(2,1)} collective-permute-done((bf16[512,256]{1,0:T(8,128)(2,1)S(1)}, bf16[512,256]{1,0:T(8,128)(2,1)}, u32[]{:S(2)}, u32[]{:S(2)}) %collective-permute-start.3) | collective-permute-done | bytes 262176 | tf_op jit(solution)/shard_map/ppermute | solution.py:321
  52.8 5.1 %collective-permute-start.12 = (bf16[512,256]{1,0:T(8,128)(2,1)}, bf16[512,256]{1,0:T(8,128)(2,1)S(1)}, u32[]{:S(2)}, u32[]{:S(2)}) collective-permute-start(bf16[512,256]{1,0:T(8,128)(2,1)} %collective-permute-done.10.refs_9_), channel_id=1, source_target_pairs={{0,8},{8,16},{16,24},{24,28},{28,20},{20,12},{12,4},{4,0},{1,9},{9... | collective-permute-start | bytes 786440 | tf_op jit(solution)/shard_map/ppermute | solution.py:321
  57.9 6.5 %collective-permute-done.11.refs_10_ = bf16[512,256]{1,0:T(8,128)(2,1)} collective-permute-done((bf16[512,256]{1,0:T(8,128)(2,1)}, bf16[512,256]{1,0:T(8,128)(2,1)}, u32[]{:S(2)}, u32[]{:S(2)}) %collective-permute-start.11) | collective-permute-done | bytes 262176 | tf_op jit(solution)/shard_map/ppermute | solution.py:321
  68.6 2.1 collective-permute-start.6
  85.0 23.8 %attention_forward.2 = (bf16[512,640]{1,0:T(8,128)(2,1)}, f32[4,640,128]{2,1,0:T(8,128)}, bf16[4608,128]{1,0:T(8,128)(2,1)}, bf16[4608,128]{1,0:T(8,128)(2,1)}) custom-call(s32[4,18]{1,0:T(4,128)} %get-tuple-element.29.refs_0_.order_ref, s32[4]{0:T(128)} %copy-done.12, s32[32]{0:T(128)} %section_ref.3, f32[4]{0:T(128)} %sqrt.3.refs_3_.root_ref, ...), custom_call_target="tpu_custom_call" | custom-call | flops 3019898880 | bytes 8388608 | tf_op jit(solution)/shard_map/attention_forward/pallas_call | solution.py:221
  108.9 23.9 %attention_forward.3 = (bf16[512,640]{1,0:T(8,128)(2,1)}, f32[4,640,128]{2,1,0:T(8,128)}, bf16[4608,128]{1,0:T(8,128)(2,1)}, bf16[4608,128]{1,0:T(8,128)(2,1)}) custom-call(s32[4,18]{1,0:T(4,128)} %get-tuple-element.29.refs_0_.order_ref, s32[4]{0:T(128)} %copy-done.12, s32[32]{0:T(128)} %section_ref.3, f32[4]{0:T(128)} %sqrt.3.refs_3_.root_ref, ...), custom_call_target="tpu_custom_call" | custom-call | flops 3019898880 | bytes 8388608 | tf_op jit(solution)/shard_map/attention_forward/pallas_call | solution.py:221
  132.8 2.2 pad_maximum_fusion.1.attn_ref
  135.0 3.2 %pad_maximum_fusion.left_ref = bf16[4,512,640]{2,1,0:T(8,128)(2,1)} fusion(bf16[2,512,640]{2,1,0:T(8,128)(2,1)} %collective-permute-done.19, bf16[1,512,640]{2,1,0:T(8,128)(2,1)S(1)} %collective-permute-done.18, bf16[1,512,640]{2,1,0:T(8,128)(2,1)S(1)} %bitcast.21), kind=kLoop, calls=%fused_computation | loop fusion | flops 2621440 | bytes 5242880 | tf_op jit(solution)/shard_map/concatenate | solution.py:410
  140.1 8.3 %cotangent_of_attn.1.grad_ref = bf16[512,1280]{1,0:T(8,128)(2,1)} custom-call(s32[1]{0:T(128)} %bitcast.me_ref, bf16[4,512,640]{2,1,0:T(8,128)(2,1)} %pad_maximum_fusion.left_ref, bf16[2560,1280]{1,0:T(8,128)(2,1)} %all-gather.2.cloned.1.call-done.weight_ref.right_ref), custom_call_target="tpu_custom_call" | custom-call | flops 3355443200 | bytes 10485760 | tf_op jit(solution)/shard_map/cotangent_of_attn/pallas_call | solution.py:441
  148.4 25.6 %attention_backward.2 = (bf16[512,640]{1,0:T(8,128)(2,1)}, bf16[4096,256]{1,0:T(8,128)(2,1)}) custom-call(s32[4,18]{1,0:T(4,128)} %get-tuple-element.29.refs_0_.order_ref, s32[4]{0:T(128)} %copy-done.12, s32[32]{0:T(128)} %section_ref.3, s32[4,18]{1,0:T(4,128)} %get-tuple-element.28.rounded_ref, f32[4]{0:T(128)} %sqrt.3.refs_3_.root_ref, ...), custom_call_target="tpu_custom_call" | custom-call | flops 7549747200 | bytes 16777216 | tf_op jit(solution)/shard_map/attention_backward/pallas_call | solution.py:268
  175.1 4.3 %collective-permute-start.20 = (bf16[256,256]{1,0:T(8,128)(2,1)S(1)}, bf16[256,256]{1,0:T(8,128)(2,1)S(1)}, u32[]{:S(2)}, u32[]{:S(2)}) collective-permute-start(bf16[256,256]{1,0:T(8,128)(2,1)S(1)} %get-tuple-element.36), channel_id=1, source_target_pairs={{0,8},{8,16},{16,24},{24,28},{28,20},{20,12},{12,4},{4,0},{1,9},{9... | collective-permute-start | bytes 393224 | tf_op jit(solution)/shard_map/ppermute | solution.py:321
  179.4 25.6 %attention_backward.3 = (bf16[512,640]{1,0:T(8,128)(2,1)}, bf16[4096,256]{1,0:T(8,128)(2,1)}) custom-call(s32[4,18]{1,0:T(4,128)} %get-tuple-element.29.refs_0_.order_ref, s32[4]{0:T(128)} %copy-done.12, s32[32]{0:T(128)} %section_ref.3, s32[4,18]{1,0:T(4,128)} %get-tuple-element.28.rounded_ref, f32[4]{0:T(128)} %sqrt.3.refs_3_.root_ref, ...), custom_call_target="tpu_custom_call" | custom-call | flops 7549747200 | bytes 16777216 | tf_op jit(solution)/shard_map/attention_backward/pallas_call | solution.py:268
  206.1 7.0 %collective-permute-start.28 = (bf16[256,256]{1,0:T(8,128)(2,1)S(1)}, bf16[256,256]{1,0:T(8,128)(2,1)S(1)}, u32[]{:S(2)}, u32[]{:S(2)}) collective-permute-start(bf16[256,256]{1,0:T(8,128)(2,1)S(1)} %get-tuple-element.44), channel_id=1, source_target_pairs={{0,8},{8,16},{16,24},{24,28},{28,20},{20,12},{12,4},{4,0},{1,9},{9... | collective-permute-start | bytes 393224 | tf_op jit(solution)/shard_map/ppermute | solution.py:321
  214.9 3.5 %collective-permute-start.21 = (bf16[512,256]{1,0:T(8,128)(2,1)S(1)}, bf16[512,256]{1,0:T(8,128)(2,1)S(1)}, u32[]{:S(2)}, u32[]{:S(2)}) collective-permute-start(bf16[512,256]{1,0:T(8,128)(2,1)S(1)} %pad_maximum_fusion.6), channel_id=1, source_target_pairs={{0,8},{8,16},{16,24},{24,28},{28,20},{20,12},{12,4},{4,0},{1,9},{9... | collective-permute-start | bytes 786440 | tf_op jit(solution)/shard_map/ppermute | solution.py:321
  228.9 2.1 collective-permute-done.29
  234.5 8.1 %projection_parts.1 = bf16[4,512,640]{2,1,0:T(8,128)(2,1)} custom-call(s32[1]{0:T(128)} %bitcast.me_ref, bf16[512,1280]{1,0:T(8,128)(2,1)} %pad_maximum_fusion.1.attn_ref, bf16[2560,1280]{1,0:T(8,128)(2,1)} %all-gather.2.cloned.1.call-done.weight_ref.right_ref), custom_call_target="tpu_custom_call" | custom-call | flops 3355443200 | bytes 10485760 | tf_op jit(solution)/shard_map/projection_parts/pallas_call | solution.py:471
  247.8 2.3 collective-permute-start.26
  250.1 2.1 add_convert_fusion.5
  252.2 2.0 collective-permute-start.34
  254.8 3.0 %collective-permute-done.26 = bf16[512,256]{1,0:T(8,128)(2,1)} collective-permute-done((bf16[512,256]{1,0:T(8,128)(2,1)}, bf16[512,256]{1,0:T(8,128)(2,1)}, u32[]{:S(2)}, u32[]{:S(2)}) %collective-permute-start.26) | collective-permute-done | bytes 262176 | tf_op jit(solution)/shard_map/ppermute | solution.py:321
  260.1 2.3 collective-permute-done.34
  263.9 2.6 pad_maximum_fusion.3
  266.6 3.6 %collective-permute-done.35 = bf16[512,256]{1,0:T(8,128)(2,1)S(1)} collective-permute-done((bf16[512,256]{1,0:T(8,128)(2,1)S(1)}, bf16[512,256]{1,0:T(8,128)(2,1)S(1)}, u32[]{:S(2)}, u32[]{:S(2)}) %collective-permute-start.35) | collective-permute-done | bytes 262176 | tf_op jit(solution)/shard_map/ppermute | solution.py:321
  (163 shorter events, 49.7 us)
Async XLA Ops:
  7.2 132.8 %all-gather.2.cloned.1.call-start = ((), (), s32[]{:S(2)}) async-start(), calls=%async_computation | async-start | bytes 7372800 | tf_op jit(solution)/shard_map/all_gather | solution.py:519
  9.2 10.2 %collective-permute-start = (bf16[512,256]{1,0:T(8,128)(2,1)S(1)}, bf16[512,256]{1,0:T(8,128)(2,1)S(1)}, u32[]{:S(2)}, u32[]{:S(2)}) collective-permute-start(bf16[512,256]{1,0:T(8,128)(2,1)S(1)} %pad_maximum_fusion.4.refs_6_), channel_id=1, source_target_pairs={{0,8},{8,16},{16,24},{24,28},{28,20},{20,12},{12,4},{4,0},{1,9},{9... | collective-permute-start | bytes 786440 | tf_op jit(solution)/shard_map/ppermute | solution.py:321
  12.3 14.7 %collective-permute-start.8 = (bf16[512,256]{1,0:T(8,128)(2,1)S(1)}, bf16[512,256]{1,0:T(8,128)(2,1)S(1)}, u32[]{:S(2)}, u32[]{:S(2)}) collective-permute-start(bf16[512,256]{1,0:T(8,128)(2,1)S(1)} %pad_maximum_fusion.5.refs_6_), channel_id=1, source_target_pairs={{0,8},{8,16},{16,24},{24,28},{28,20},{20,12},{12,4},{4,0},{1,9},{9... | collective-permute-start | bytes 786440 | tf_op jit(solution)/shard_map/ppermute | solution.py:321
  14.4 17.9 %collective-permute-start.9 = (bf16[512,256]{1,0:T(8,128)(2,1)S(1)}, bf16[512,256]{1,0:T(8,128)(2,1)}, u32[]{:S(2)}, u32[]{:S(2)}) collective-permute-start(bf16[512,256]{1,0:T(8,128)(2,1)S(1)} %pad_maximum_fusion.5.refs_6_), channel_id=1, source_target_pairs={{0,4},{8,0},{16,8},{24,16},{28,24},{20,28},{12,20},{4,12},{1,5},{9... | collective-permute-start | bytes 786440 | tf_op jit(solution)/shard_map/ppermute | solution.py:321
  14.4 35.5 %collective-permute-start.18 = (bf16[1,512,640]{2,1,0:T(8,128)(2,1)S(1)}, bf16[1,512,640]{2,1,0:T(8,128)(2,1)S(1)}, u32[]{:S(2)}, u32[]{:S(2)}) collective-permute-start(bf16[1,512,640]{2,1,0:T(8,128)(2,1)S(1)} %bitcast.19), channel_id=1, source_target_pairs={{0,1},{1,0},{2,3},{3,2},{4,5},{5,4},{6,7},{7,6},{8,9},{9,8},{10,11... | collective-permute-start | bytes 1966088 | tf_op jit(solution)/shard_map/ppermute | solution.py:403
  19.4 18.9 %collective-permute-start.2 = (bf16[512,256]{1,0:T(8,128)(2,1)S(1)}, bf16[512,256]{1,0:T(8,128)(2,1)}, u32[]{:S(2)}, u32[]{:S(2)}) collective-permute-start(bf16[512,256]{1,0:T(8,128)(2,1)S(1)} %collective-permute-done.refs_7_), channel_id=1, source_target_pairs={{0,8},{8,16},{16,24},{24,28},{28,20},{20,12},{12,4},{4,0},{1,9},{9... | collective-permute-start | bytes 786440 | tf_op jit(solution)/shard_map/ppermute | solution.py:321
  21.5 28.4 %collective-permute-start.3 = (bf16[512,256]{1,0:T(8,128)(2,1)S(1)}, bf16[512,256]{1,0:T(8,128)(2,1)}, u32[]{:S(2)}, u32[]{:S(2)}) collective-permute-start(bf16[512,256]{1,0:T(8,128)(2,1)S(1)} %collective-permute-done.1.refs_8_), channel_id=1, source_target_pairs={{0,4},{8,0},{16,8},{24,16},{28,24},{20,28},{12,20},{4,12},{1,5},{9... | collective-permute-start | bytes 786440 | tf_op jit(solution)/shard_map/ppermute | solution.py:321
  27.0 25.8 %collective-permute-start.10 = (bf16[512,256]{1,0:T(8,128)(2,1)S(1)}, bf16[512,256]{1,0:T(8,128)(2,1)}, u32[]{:S(2)}, u32[]{:S(2)}) collective-permute-start(bf16[512,256]{1,0:T(8,128)(2,1)S(1)} %collective-permute-done.8.refs_7_), channel_id=1, source_target_pairs={{0,8},{8,16},{16,24},{24,28},{28,20},{20,12},{12,4},{4,0},{1,9},{9... | collective-permute-start | bytes 786440 | tf_op jit(solution)/shard_map/ppermute | solution.py:321
  32.3 32.2 %collective-permute-start.11 = (bf16[512,256]{1,0:T(8,128)(2,1)}, bf16[512,256]{1,0:T(8,128)(2,1)}, u32[]{:S(2)}, u32[]{:S(2)}) collective-permute-start(bf16[512,256]{1,0:T(8,128)(2,1)} %collective-permute-done.9.refs_8_), channel_id=1, source_target_pairs={{0,4},{8,0},{16,8},{24,16},{28,24},{20,28},{12,20},{4,12},{1,5},{9... | collective-permute-start | bytes 786440 | tf_op jit(solution)/shard_map/ppermute | solution.py:321
  38.3 30.3 %collective-permute-start.4 = (bf16[512,256]{1,0:T(8,128)(2,1)}, bf16[512,256]{1,0:T(8,128)(2,1)S(1)}, u32[]{:S(2)}, u32[]{:S(2)}) collective-permute-start(bf16[512,256]{1,0:T(8,128)(2,1)} %collective-permute-done.2.refs_9_), channel_id=1, source_target_pairs={{0,8},{8,16},{16,24},{24,28},{28,20},{20,12},{12,4},{4,0},{1,9},{9... | collective-permute-start | bytes 786440 | tf_op jit(solution)/shard_map/ppermute | solution.py:321
  49.9 20.8 %collective-permute-start.5 = (bf16[512,256]{1,0:T(8,128)(2,1)}, bf16[512,256]{1,0:T(8,128)(2,1)S(1)}, u32[]{:S(2)}, u32[]{:S(2)}) collective-permute-start(bf16[512,256]{1,0:T(8,128)(2,1)} %collective-permute-done.3.refs_10_), channel_id=1, source_target_pairs={{0,4},{8,0},{16,8},{24,16},{28,24},{20,28},{12,20},{4,12},{1,5},{9... | collective-permute-start | bytes 786440 | tf_op jit(solution)/shard_map/ppermute | solution.py:321
  51.2 83.8 %collective-permute-start.19 = (bf16[2,512,640]{2,1,0:T(8,128)(2,1)}, bf16[2,512,640]{2,1,0:T(8,128)(2,1)}, u32[]{:S(2)}, u32[]{:S(2)}) collective-permute-start(bf16[2,512,640]{2,1,0:T(8,128)(2,1)} %pad_maximum_fusion.2), channel_id=1, source_target_pairs={{0,2},{1,3},{2,0},{3,1},{4,6},{5,7},{6,4},{7,5},{8,10},{9,11},{10,... | collective-permute-start | bytes 3932168 | tf_op jit(solution)/shard_map/ppermute | solution.py:403
  52.8 28.1 %collective-permute-start.12 = (bf16[512,256]{1,0:T(8,128)(2,1)}, bf16[512,256]{1,0:T(8,128)(2,1)S(1)}, u32[]{:S(2)}, u32[]{:S(2)}) collective-permute-start(bf16[512,256]{1,0:T(8,128)(2,1)} %collective-permute-done.10.refs_9_), channel_id=1, source_target_pairs={{0,8},{8,16},{16,24},{24,28},{28,20},{20,12},{12,4},{4,0},{1,9},{9... | collective-permute-start | bytes 786440 | tf_op jit(solution)/shard_map/ppermute | solution.py:321
  64.4 19.2 %collective-permute-start.13 = (bf16[512,256]{1,0:T(8,128)(2,1)}, bf16[512,256]{1,0:T(8,128)(2,1)S(1)}, u32[]{:S(2)}, u32[]{:S(2)}) collective-permute-start(bf16[512,256]{1,0:T(8,128)(2,1)} %collective-permute-done.11.refs_10_), channel_id=1, source_target_pairs={{0,4},{8,0},{16,8},{24,16},{28,24},{20,28},{12,20},{4,12},{1,5},{9... | collective-permute-start | bytes 786440 | tf_op jit(solution)/shard_map/ppermute | solution.py:321
  68.6 15.8 %collective-permute-start.6 = (bf16[256,256]{1,0:T(8,128)(2,1)S(1)}, bf16[256,256]{1,0:T(8,128)(2,1)S(1)}, u32[]{:S(2)}, u32[]{:S(2)}) collective-permute-start(bf16[256,256]{1,0:T(8,128)(2,1)S(1)} %slice.112), channel_id=1, source_target_pairs={{0,8},{8,16},{16,24},{24,28},{28,20},{20,12},{12,4},{4,0},{1,9},{9... | collective-permute-start | bytes 393224 | tf_op jit(solution)/shard_map/ppermute | solution.py:321
  70.7 13.7 %collective-permute-start.7 = (bf16[256,256]{1,0:T(8,128)(2,1)S(1)}, bf16[256,256]{1,0:T(8,128)(2,1)}, u32[]{:S(2)}, u32[]{:S(2)}) collective-permute-start(bf16[256,256]{1,0:T(8,128)(2,1)S(1)} %slice.113), channel_id=1, source_target_pairs={{0,4},{8,0},{16,8},{24,16},{28,24},{20,28},{12,20},{4,12},{1,5},{9... | collective-permute-start | bytes 393224 | tf_op jit(solution)/shard_map/ppermute | solution.py:321
  81.6 27.2 %collective-permute-start.14 = (bf16[256,256]{1,0:T(8,128)(2,1)}, bf16[256,256]{1,0:T(8,128)(2,1)}, u32[]{:S(2)}, u32[]{:S(2)}) collective-permute-start(bf16[256,256]{1,0:T(8,128)(2,1)} %slice.114), channel_id=1, source_target_pairs={{0,8},{8,16},{16,24},{24,28},{28,20},{20,12},{12,4},{4,0},{1,9},{9... | collective-permute-start | bytes 393224 | tf_op jit(solution)/shard_map/ppermute | solution.py:321
  84.3 24.6 %collective-permute-start.15 = (bf16[256,256]{1,0:T(8,128)(2,1)}, bf16[256,256]{1,0:T(8,128)(2,1)}, u32[]{:S(2)}, u32[]{:S(2)}) collective-permute-start(bf16[256,256]{1,0:T(8,128)(2,1)} %slice.115), channel_id=1, source_target_pairs={{0,4},{8,0},{16,8},{24,16},{28,24},{20,28},{12,20},{4,12},{1,5},{9... | collective-permute-start | bytes 393224 | tf_op jit(solution)/shard_map/ppermute | solution.py:321
  175.1 38.0 %collective-permute-start.20 = (bf16[256,256]{1,0:T(8,128)(2,1)S(1)}, bf16[256,256]{1,0:T(8,128)(2,1)S(1)}, u32[]{:S(2)}, u32[]{:S(2)}) collective-permute-start(bf16[256,256]{1,0:T(8,128)(2,1)S(1)} %get-tuple-element.36), channel_id=1, source_target_pairs={{0,8},{8,16},{16,24},{24,28},{28,20},{20,12},{12,4},{4,0},{1,9},{9... | collective-permute-start | bytes 393224 | tf_op jit(solution)/shard_map/ppermute | solution.py:321
  179.4 33.7 %collective-permute-start.24 = (bf16[256,256]{1,0:T(8,128)(2,1)S(1)}, bf16[256,256]{1,0:T(8,128)(2,1)S(1)}, u32[]{:S(2)}, u32[]{:S(2)}) collective-permute-start(bf16[256,256]{1,0:T(8,128)(2,1)S(1)} %get-tuple-element.38), channel_id=1, source_target_pairs={{0,4},{8,0},{16,8},{24,16},{28,24},{20,28},{12,20},{4,12},{1,5},{9... | collective-permute-start | bytes 393224 | tf_op jit(solution)/shard_map/ppermute | solution.py:321
  206.1 12.4 %collective-permute-start.28 = (bf16[256,256]{1,0:T(8,128)(2,1)S(1)}, bf16[256,256]{1,0:T(8,128)(2,1)S(1)}, u32[]{:S(2)}, u32[]{:S(2)}) collective-permute-start(bf16[256,256]{1,0:T(8,128)(2,1)S(1)} %get-tuple-element.44), channel_id=1, source_target_pairs={{0,8},{8,16},{16,24},{24,28},{28,20},{20,12},{12,4},{4,0},{1,9},{9... | collective-permute-start | bytes 393224 | tf_op jit(solution)/shard_map/ppermute | solution.py:321
  214.9 31.0 %collective-permute-start.25 = (bf16[512,256]{1,0:T(8,128)(2,1)}, bf16[512,256]{1,0:T(8,128)(2,1)}, u32[]{:S(2)}, u32[]{:S(2)}) collective-permute-start(bf16[512,256]{1,0:T(8,128)(2,1)} %pad_maximum_fusion.7), channel_id=1, source_target_pairs={{0,4},{8,0},{16,8},{24,16},{28,24},{20,28},{12,20},{4,12},{1,5},{9... | collective-permute-start | bytes 786440 | tf_op jit(solution)/shard_map/ppermute | solution.py:321
  214.9 10.7 %collective-permute-start.21 = (bf16[512,256]{1,0:T(8,128)(2,1)S(1)}, bf16[512,256]{1,0:T(8,128)(2,1)S(1)}, u32[]{:S(2)}, u32[]{:S(2)}) collective-permute-start(bf16[512,256]{1,0:T(8,128)(2,1)S(1)} %pad_maximum_fusion.6), channel_id=1, source_target_pairs={{0,8},{8,16},{16,24},{24,28},{28,20},{20,12},{12,4},{4,0},{1,9},{9... | collective-permute-start | bytes 786440 | tf_op jit(solution)/shard_map/ppermute | solution.py:321
  220.9 10.2 %collective-permute-start.29 = (bf16[512,256]{1,0:T(8,128)(2,1)S(1)}, bf16[512,256]{1,0:T(8,128)(2,1)S(1)}, u32[]{:S(2)}, u32[]{:S(2)}) collective-permute-start(bf16[512,256]{1,0:T(8,128)(2,1)S(1)} %pad_maximum_fusion.8), channel_id=1, source_target_pairs={{0,8},{8,16},{16,24},{24,28},{28,20},{20,12},{12,4},{4,0},{1,9},{9... | collective-permute-start | bytes 786440 | tf_op jit(solution)/shard_map/ppermute | solution.py:321
  223.4 26.7 %collective-permute-start.33 = (bf16[512,256]{1,0:T(8,128)(2,1)}, bf16[512,256]{1,0:T(8,128)(2,1)}, u32[]{:S(2)}, u32[]{:S(2)}) collective-permute-start(bf16[512,256]{1,0:T(8,128)(2,1)} %pad_maximum_fusion.9), channel_id=1, source_target_pairs={{0,4},{8,0},{16,8},{24,16},{28,24},{20,28},{12,20},{4,12},{1,5},{9... | collective-permute-start | bytes 786440 | tf_op jit(solution)/shard_map/ppermute | solution.py:321
  227.3 18.6 %collective-permute-start.22 = (bf16[512,256]{1,0:T(8,128)(2,1)}, bf16[512,256]{1,0:T(8,128)(2,1)}, u32[]{:S(2)}, u32[]{:S(2)}) collective-permute-start(bf16[512,256]{1,0:T(8,128)(2,1)} %add_convert_fusion.11), channel_id=1, source_target_pairs={{0,8},{8,16},{16,24},{24,28},{28,20},{20,12},{12,4},{4,0},{1,9},{9... | collective-permute-start | bytes 786440 | tf_op jit(solution)/shard_map/ppermute | solution.py:321
  232.8 17.4 %collective-permute-start.30 = (bf16[512,256]{1,0:T(8,128)(2,1)}, bf16[512,256]{1,0:T(8,128)(2,1)}, u32[]{:S(2)}, u32[]{:S(2)}) collective-permute-start(bf16[512,256]{1,0:T(8,128)(2,1)} %add_convert_fusion.6), channel_id=1, source_target_pairs={{0,8},{8,16},{16,24},{24,28},{28,20},{20,12},{12,4},{4,0},{1,9},{9... | collective-permute-start | bytes 786440 | tf_op jit(solution)/shard_map/ppermute | solution.py:321
  244.2 27.0 %collective-permute-start.16 = (bf16[2,512,640]{2,1,0:T(8,128)(2,1)S(1)}, bf16[2,512,640]{2,1,0:T(8,128)(2,1)}, u32[]{:S(2)}, u32[]{:S(2)}) collective-permute-start(bf16[2,512,640]{2,1,0:T(8,128)(2,1)S(1)} %slice.117), channel_id=1, source_target_pairs={{0,2},{1,3},{2,0},{3,1},{4,6},{5,7},{6,4},{7,5},{8,10},{9,11},{10,... | collective-permute-start | bytes 3932168 | tf_op jit(solution)/shard_map/ppermute | solution.py:403
  247.8 10.0 %collective-permute-start.26 = (bf16[512,256]{1,0:T(8,128)(2,1)}, bf16[512,256]{1,0:T(8,128)(2,1)}, u32[]{:S(2)}, u32[]{:S(2)}) collective-permute-start(bf16[512,256]{1,0:T(8,128)(2,1)} %get-tuple-element.33), channel_id=1, source_target_pairs={{0,4},{8,0},{16,8},{24,16},{28,24},{20,28},{12,20},{4,12},{1,5},{9... | collective-permute-start | bytes 786440 | tf_op jit(solution)/shard_map/ppermute | solution.py:321
  252.2 10.2 %collective-permute-start.34 = (bf16[512,256]{1,0:T(8,128)(2,1)}, bf16[512,256]{1,0:T(8,128)(2,1)}, u32[]{:S(2)}, u32[]{:S(2)}) collective-permute-start(bf16[512,256]{1,0:T(8,128)(2,1)} %get-tuple-element.41), channel_id=1, source_target_pairs={{0,4},{8,0},{16,8},{24,16},{28,24},{20,28},{12,20},{4,12},{1,5},{9... | collective-permute-start | bytes 786440 | tf_op jit(solution)/shard_map/ppermute | solution.py:321
  254.3 12.2 %collective-permute-start.23 = (bf16[512,256]{1,0:T(8,128)(2,1)}, bf16[512,256]{1,0:T(8,128)(2,1)S(1)}, u32[]{:S(2)}, u32[]{:S(2)}) collective-permute-start(bf16[512,256]{1,0:T(8,128)(2,1)} %get-tuple-element.32), channel_id=1, source_target_pairs={{0,8},{8,16},{16,24},{24,28},{28,20},{20,12},{12,4},{4,0},{1,9},{9... | collective-permute-start | bytes 786440 | tf_op jit(solution)/shard_map/ppermute | solution.py:321
  254.3 12.3 %collective-permute-start.31 = (bf16[512,256]{1,0:T(8,128)(2,1)}, bf16[512,256]{1,0:T(8,128)(2,1)S(1)}, u32[]{:S(2)}, u32[]{:S(2)}) collective-permute-start(bf16[512,256]{1,0:T(8,128)(2,1)} %get-tuple-element.40), channel_id=1, source_target_pairs={{0,8},{8,16},{16,24},{24,28},{28,20},{20,12},{12,4},{4,0},{1,9},{9... | collective-permute-start | bytes 786440 | tf_op jit(solution)/shard_map/ppermute | solution.py:321
  (27 other events, 578.2 us)
Sparse Core Ops, SparseCore 0:
  10.2 129.8 all-gather.1

commit v3 on v1

v3 whole, which is shorter than its diff:
```python
import functools
import math

import jax
import jax.numpy as jnp
import numpy as np
from jax import lax
from jax.experimental import pallas as pl
from jax.experimental.pallas import tpu as pltpu
from jax.sharding import PartitionSpec as P

HEAD_DIMENSION = 128
BLK = 128
LOOK = 4
ANC = 2
XREF = 12
SLOTS = LOOK + ANC + XREF
GROUP = 2

neg_large = -1e30
scaling = HEAD_DIMENSION ** (-0.5)
to_base_two = scaling * math.log2(math.e)


def rows_of(index):
    return pl.ds(pl.multiple_of(index * BLK, BLK), BLK)


def product(left, right, left_dim, right_dim):
    return lax.dot_general(
        left, right, (((left_dim,), (right_dim,)), ((), ())), preferred_element_type=jnp.float32
    )


def tile_of(ref, block, head):
    return ref[
        block * BLK : (block + 1) * BLK, head * HEAD_DIMENSION : (head + 1) * HEAD_DIMENSION
    ]


def masked_scores(scores, first_slot, valid_count, heads):
    rows = heads * BLK
    key_minus_query = lax.broadcasted_iota(jnp.int32, (BLK, BLK), 1) - lax.broadcasted_iota(
        jnp.int32, (BLK, BLK), 0
    )
    ahead = jnp.concatenate([key_minus_query] * heads, axis=0)
    pieces = []
    for w in range(GROUP):
        slot = first_slot + w
        reach = jnp.where(slot < valid_count, jnp.where(slot == 0, 0, BLK), -BLK)
        piece = scores[:, w * BLK : (w + 1) * BLK]
        pieces.append(jnp.where(ahead <= reach, piece, neg_large))
    return pieces


def extended_kernel(shard_rows, section_ref, root_ref, place_ref, *refs):
    shard_refs = refs[: len(shard_rows)]
    *targets, total_ref = refs[len(shard_rows) :]
    blocks, sections = section_ref.shape[0], root_ref.shape[0]
    for number, target in enumerate(targets):
        lanes = slice(number * HEAD_DIMENSION, (number + 1) * HEAD_DIMENSION)
        for place, (shard_ref, rows) in enumerate(zip(shard_refs, shard_rows)):
            first = pl.multiple_of(place_ref[place], BLK)
            target[pl.ds(first, rows)] = shard_ref[:, lanes]
        total_ref[...] = jnp.zeros_like(total_ref)

        @pl.loop(0, blocks)
        def _(index):
            place = rows_of(section_ref[index])
            total_ref[place] += target[rows_of(index)].astype(jnp.float32)

        @pl.loop(0, sections)
        def _(index):
            target[rows_of(blocks + index)] = (
                total_ref[rows_of(index)] / root_ref[index]
            ).astype(jnp.bfloat16)


def forward_kernel(block, head, order_ref, count_ref, query_ref, keys_ref, values_ref, *refs):
    attn_ref, lse_ref, stack_ref, score_ref, wide_ref, out_ref = refs[-6:]
    heads = attn_ref.shape[1] // HEAD_DIMENSION
    for g in range(heads):
        stack_ref[g * BLK : (g + 1) * BLK] = tile_of(query_ref, block, head * heads + g)
    query = stack_ref[...]
    valid_count = count_ref[block]
    steps = (valid_count + GROUP - 1) // GROUP

    def gathered(source, step):
        return jnp.concatenate(
            [source[rows_of(order_ref[block, step * GROUP + w])] for w in range(GROUP)], axis=0
        )

    wide_ref[...] = jnp.full_like(wide_ref, neg_large)

    @pl.loop(0, steps)
    def _(step):
        scores = product(query, gathered(keys_ref, step), 1, 1)
        pieces = masked_scores(scores, step * GROUP, valid_count, heads)
        largest = wide_ref[...]
        for w, piece in enumerate(pieces):
            score_ref[step, :, w * BLK : (w + 1) * BLK] = piece
            largest = jnp.maximum(largest, piece)
        wide_ref[...] = largest

    largest = jnp.max(wide_ref[...], axis=1, keepdims=True) * to_base_two
    wide_ref[...] = jnp.zeros_like(wide_ref)

    @pl.loop(0, steps)
    def _(step):
        exponent = jnp.exp2(score_ref[step] * to_base_two - largest)
        score_ref[step] = exponent
        total = wide_ref[...]
        for w in range(GROUP):
            total = total + exponent[:, w * BLK : (w + 1) * BLK]
        wide_ref[...] = total

    total = jnp.sum(wide_ref[...], axis=1, keepdims=True)
    lse_ref[...] = jnp.broadcast_to(largest + jnp.log2(total), lse_ref.shape)
    inverse = 1.0 / total
    out_ref[...] = jnp.zeros_like(out_ref)

    @pl.loop(0, steps)
    def _(step):
        light = (score_ref[step] * inverse).astype(jnp.bfloat16)
        out_ref[...] += product(light, gathered(values_ref, step), 1, 0)

    for g in range(heads):
        attn_ref[:, g * HEAD_DIMENSION : (g + 1) * HEAD_DIMENSION] = out_ref[
            g * BLK : (g + 1) * BLK
        ].astype(jnp.bfloat16)


def backward_kernel(
    numbers, head, first, last, far,
    section_ref, root_ref, order_ref, count_ref, rounded_ref, place_ref,
    query_ref, grad_ref, keys_ref, values_ref, *refs
):
    number = len(numbers)
    *outs, query_stack, grad_stack, delta_ref, sum_ref = refs[2 * number :]
    outs = outs[-(number + 5) :] if last else outs[-(number + 2) :]
    key_sum_ref, value_sum_ref = outs[number : number + 2]
    if first:
        key_sum_ref[...] = jnp.zeros_like(key_sum_ref)
        value_sum_ref[...] = jnp.zeros_like(value_sum_ref)
    for i, block in enumerate(numbers):
        backward_block(
            block, head, order_ref, count_ref, rounded_ref,
            query_ref, grad_ref, *refs[2 * i : 2 * i + 2],
            keys_ref, values_ref, outs[i], key_sum_ref, value_sum_ref,
            query_stack, grad_stack, delta_ref, sum_ref,
        )
    if last:
        terms_ref, ahead_ref, back_ref = outs[-3:]
        blocks = section_ref.shape[0]

        @pl.loop(0, blocks)
        def _(index):
            section = section_ref[index]
            root = root_ref[section]
            for half, source in enumerate((key_sum_ref, value_sum_ref)):
                lanes = slice(half * HEAD_DIMENSION, (half + 1) * HEAD_DIMENSION)
                total = source[rows_of(index)] + source[rows_of(blocks + section)] / root
                terms_ref[rows_of(index), lanes] = total.astype(jnp.bfloat16)

        half = ahead_ref.shape[0]
        start = pl.multiple_of(place_ref[far], BLK)
        ahead_ref[...] = terms_ref[pl.ds(start, half)]
        back_ref[...] = terms_ref[pl.ds(start + half, half)]


def backward_block(
    block, head, order_ref, count_ref, rounded_ref, query_ref, grad_ref, attn_ref, lse_ref,
    keys_ref, values_ref, grad_query_ref, key_sum_ref, value_sum_ref,
    query_stack, grad_stack, delta_ref, sum_ref,
):
    heads = attn_ref.shape[1] // HEAD_DIMENSION
    for g in range(heads):
        lanes = slice(g * HEAD_DIMENSION, (g + 1) * HEAD_DIMENSION)
        rows = slice(g * BLK, (g + 1) * BLK)
        query_stack[rows] = tile_of(query_ref, block, head * heads + g)
        grad = tile_of(grad_ref, block, g)
        grad_stack[rows] = grad
        delta = jnp.sum(
            grad.astype(jnp.float32) * attn_ref[:, lanes].astype(jnp.float32), axis=1, keepdims=True
        )
        delta_ref[rows] = jnp.broadcast_to(delta, (BLK, BLK))
    query = query_stack[...]
    grad = grad_stack[...]
    valid_count = count_ref[block]
    steps = (valid_count + GROUP - 1) // GROUP
    sum_ref[...] = jnp.zeros_like(sum_ref)

    @pl.loop(0, steps)
    def _(step):
        places = [order_ref[block, step * GROUP + w] for w in range(GROUP)]
        keys = jnp.concatenate([keys_ref[rows_of(place)] for place in places], axis=0)
        values = jnp.concatenate([values_ref[rows_of(place)] for place in places], axis=0)
        scores = product(query, keys, 1, 1)
        d_weights = product(grad, values, 1, 1)
        lse = lse_ref[...]
        delta = delta_ref[...]
        light, d_scores = [], []
        for w, piece in enumerate(masked_scores(scores, step * GROUP, valid_count, heads)):
            weights = jnp.exp2(piece * to_base_two - lse)
            light.append(weights.astype(jnp.bfloat16))
            slope = d_weights[:, w * BLK : (w + 1) * BLK] - delta
            d_scores.append((weights * slope * scaling).astype(jnp.bfloat16))
        light = jnp.concatenate(light, axis=1)
        d_scores = jnp.concatenate(d_scores, axis=1)
        sum_ref[...] += product(d_scores, keys, 1, 0)
        key_terms = product(d_scores, query, 0, 0)
        value_terms = product(light, grad, 0, 0)
        for w, place in enumerate(places):
            rounds = rounded_ref[block, step * GROUP + w] > 0
            for terms, target in ((key_terms, key_sum_ref), (value_terms, value_sum_ref)):
                term = terms[w * BLK : (w + 1) * BLK]
                term = jnp.where(rounds, term.astype(jnp.bfloat16).astype(jnp.float32), term)
                target[rows_of(place)] += term

    for g in range(heads):
        grad_query_ref[:, g * HEAD_DIMENSION : (g + 1) * HEAD_DIMENSION] = sum_ref[
            g * BLK : (g + 1) * BLK
        ].astype(jnp.bfloat16)


smem = pl.BlockSpec(memory_space=pltpu.SMEM)
vmem = pl.BlockSpec(memory_space=pltpu.VMEM)
anywhere = pl.BlockSpec(memory_space=pl.ANY)


def bytes_of(*arrays):
    return sum(math.prod(array.shape) * array.dtype.itemsize for array in arrays)


def params(*arrays):
    limit = min(bytes_of(*arrays) + (20 << 20), 62 << 20)
    return pltpu.CompilerParams(vmem_limit_bytes=limit)


def extended_blocks(shards, places, block_section, root_counts):
    extended = (block_section.shape[0] + root_counts.shape[0]) * BLK
    count = shards[0].shape[1] // HEAD_DIMENSION
    outs = [jax.ShapeDtypeStruct((extended, HEAD_DIMENSION), jnp.bfloat16)] * count
    return pl.pallas_call(
        functools.partial(extended_kernel, [shard.shape[0] for shard in shards]),
        name="extended_blocks",
        in_specs=[smem] * 3 + [vmem] * len(shards),
        out_specs=[vmem] * count,
        out_shape=outs,
        scratch_shapes=[pltpu.VMEM((root_counts.shape[0] * BLK, HEAD_DIMENSION), jnp.float32)],
        compiler_params=params(*shards, *outs),
        cost_estimate=pl.CostEstimate(
            flops=bytes_of(*outs), bytes_accessed=3 * bytes_of(*outs), transcendentals=0
        ),
    )(block_section, root_counts, places, *shards)


def attention_forward(block, head, width, queries, keys, values, order, count, after):
    rows = width // HEAD_DIMENSION * BLK
    matmul = 2 * SLOTS * BLK * BLK * width
    outs = [
        jax.ShapeDtypeStruct((BLK, width), jnp.bfloat16),
        jax.ShapeDtypeStruct((rows, HEAD_DIMENSION), jnp.float32),
    ]
    scores = jax.ShapeDtypeStruct((-(-SLOTS // GROUP), rows, GROUP * BLK), jnp.float32)
    return pl.pallas_call(
        functools.partial(forward_kernel, block, head),
        name="attention_forward",
        in_specs=[smem, smem, vmem, vmem, vmem] + [anywhere] * len(after),
        out_specs=[vmem, vmem],
        out_shape=outs,
        scratch_shapes=[
            pltpu.VMEM((rows, HEAD_DIMENSION), jnp.bfloat16),
            pltpu.VMEM(scores.shape, scores.dtype),
            pltpu.VMEM((rows, HEAD_DIMENSION), jnp.float32),
            pltpu.VMEM((rows, HEAD_DIMENSION), jnp.float32),
        ],
        compiler_params=params(queries, keys, values, scores, *outs),
        cost_estimate=pl.CostEstimate(
            flops=2 * matmul, bytes_accessed=4 << 20, transcendentals=matmul // 256
        ),
    )(order, count, queries, keys, values, *after)


def attention_backward(
    numbers, head, last, ring, tables, queries, grads, forward, keys, values, sums, after
):
    number, width = len(numbers), grads.shape[1]
    rows = width // HEAD_DIMENSION * BLK
    matmul = 2 * SLOTS * BLK * BLK * width * number
    total = jax.ShapeDtypeStruct(keys.shape, jnp.float32)
    outs = [jax.ShapeDtypeStruct((BLK, width), jnp.bfloat16)] * number + [total, total]
    if last:
        tokens = queries.shape[0]
        for out_rows in (ring.size * tokens, tokens // 2, tokens // 2):
            outs.append(jax.ShapeDtypeStruct((out_rows, 2 * HEAD_DIMENSION), jnp.bfloat16))
    arrays = [queries, grads, keys, values, *[array for pair in forward for array in pair]]
    first_sum = len(tables) + len(arrays) + len(after)
    return pl.pallas_call(
        functools.partial(backward_kernel, numbers, head, not sums, last, ring.terms_at(ring.size // 2)),
        name="attention_backward",
        in_specs=[smem] * len(tables)
        + [vmem] * len(arrays)
        + [anywhere] * len(after)
        + [vmem] * len(sums),
        out_specs=[vmem] * len(outs),
        out_shape=outs,
        input_output_aliases={first_sum + i: number + i for i in range(len(sums))},
        scratch_shapes=[
            pltpu.VMEM((rows, HEAD_DIMENSION), jnp.bfloat16),
            pltpu.VMEM((rows, HEAD_DIMENSION), jnp.bfloat16),
            pltpu.VMEM((rows, HEAD_DIMENSION), jnp.float32),
            pltpu.VMEM((rows, HEAD_DIMENSION), jnp.float32),
        ],
        compiler_params=params(*arrays, *outs, *sums),
        cost_estimate=pl.CostEstimate(
            flops=5 * matmul, bytes_accessed=number * (4 << 20), transcendentals=matmul // 256
        ),
    )(*tables, *arrays, *after, *sums)


class Ring:
    def __init__(self, axis, key_rows, weight_rows):
        self.axis = axis
        self.size = size = lax.axis_size(axis)
        self.cycle = cycle = [*range(0, size, 2), *reversed(range(1, size, 2))]
        distances = [0]
        for step in range(1, size // 2):
            distances += [-step, step]
        table = np.zeros((size, 0), np.int32)
        at = np.argsort(np.array(cycle))
        cycle = np.array(cycle)
        for rows in (key_rows, weight_rows):
            whole = np.stack([cycle[(at + distance) % size] * rows for distance in distances], 1)
            far = cycle[(at + size // 2) % size][:, None] * rows + np.array([[0, rows // 2]])
            table = np.concatenate([table, whole, far], axis=1)
        self.key_places, self.weight_places = 0, size + 1
        self.term_places = table.shape[1]
        terms = np.stack([cycle[(at + distance) % size] * key_rows for distance in range(size)], 1)
        table = np.concatenate([table, terms], axis=1).astype(np.int32)
        row = lax.dynamic_slice_in_dim(jnp.asarray(table), lax.axis_index(axis), 1)
        self.places = row.reshape(-1)

    def terms_at(self, distance):
        return self.term_places + distance % self.size

    def sent(self, block, direction):
        cycle, size = self.cycle, self.size
        route = [(cycle[k], cycle[(k + direction) % size]) for k in range(size)]
        return lax.ppermute(block, self.axis, route)

    def gather(self, block):
        return Gather(self, block)


class Gather:
    def __init__(self, ring, block):
        self.ring = ring
        self.half = block.shape[0] // 2
        self.pieces = [block]
        self.ahead = self.back = block
        self.left = ring.size // 2

    def step(self, after=()):
        ahead, back = self.ahead, self.back
        if after:
            ahead, back, _ = lax.optimization_barrier((ahead, back, list(after)))
        self.left -= 1
        if not self.left:
            ahead, back = ahead[: self.half], back[self.half :]
        self.ahead, self.back = self.ring.sent(ahead, 1), self.ring.sent(back, -1)
        self.pieces += [self.ahead, self.back]
        return [self.ahead, self.back]

    def rest(self, after=()):
        while self.left:
            self.step(after)
        return self.pieces


def added_kernel(up, down, place_ref, terms_ref, ahead_in, back_in, *refs):
    ahead_ref, back_ref = refs[-2:]
    rows, half = ahead_ref.shape[0], ahead_in.shape[0]
    for place, source, target, first in (
        (up, ahead_in, ahead_ref, 0), (down, back_in, back_ref, rows - half)
    ):
        start = pl.multiple_of(place_ref[place], BLK)
        if half < rows:
            target[...] = terms_ref[pl.ds(start, rows)]
        own = terms_ref[pl.ds(start + first, half)].astype(jnp.float32)
        target[first : first + half] = (own + source[...].astype(jnp.float32)).astype(jnp.bfloat16)


def added_terms(ring, step, terms, ahead, back, after):
    out = jax.ShapeDtypeStruct((terms.shape[0] // ring.size, terms.shape[1]), jnp.bfloat16)
    return pl.pallas_call(
        functools.partial(added_kernel, ring.terms_at(step), ring.terms_at(-step)),
        name="added_terms",
        in_specs=[smem] + [vmem] * 3 + [anywhere] * len(after),
        out_specs=[vmem, vmem],
        out_shape=[out, out],
        compiler_params=params(terms, ahead, back, out, out),
        cost_estimate=pl.CostEstimate(
            flops=out.size, bytes_accessed=bytes_of(out, out, out), transcendentals=0
        ),
    )(ring.places, terms, ahead, back, *after)


class Reduction:
    def __init__(self, ring, terms, ahead, back):
        self.ring, self.terms = ring, terms
        self.moves = [ring.sent(ahead, 1), ring.sent(back, -1)]
        self.left = ring.size // 2 - 1

    def step(self, after=()):
        summed = added_terms(self.ring, self.left, self.terms, *self.moves, after)
        self.left -= 1
        self.moves = [self.ring.sent(summed[0], 1), self.ring.sent(summed[1], -1)]
        return list(summed)

    def rest(self):
        while self.left:
            self.step()
        return self.moves


def last_kernel(own, place_ref, *refs):
    d_keys_ref, d_values_ref = refs[-2:]
    start = pl.multiple_of(place_ref[own], BLK)
    for c in range(len(refs) // 3):
        terms_ref, ahead_ref, back_ref = refs[3 * c : 3 * c + 3]
        total = terms_ref[pl.ds(start, ahead_ref.shape[0])].astype(jnp.float32)
        total = total + ahead_ref[...].astype(jnp.float32) + back_ref[...].astype(jnp.float32)
        lanes = slice(c * HEAD_DIMENSION, (c + 1) * HEAD_DIMENSION)
        d_keys_ref[:, lanes] = total[:, :HEAD_DIMENSION].astype(jnp.bfloat16)
        d_values_ref[:, lanes] = total[:, HEAD_DIMENSION:].astype(jnp.bfloat16)


def last_sums(ring, arrays):
    out = jax.ShapeDtypeStruct(
        (arrays[1].shape[0], len(arrays) // 3 * HEAD_DIMENSION), jnp.bfloat16
    )
    return pl.pallas_call(
        functools.partial(last_kernel, ring.terms_at(0)),
        name="last_sums",
        in_specs=[smem] + [vmem] * len(arrays),
        out_specs=[vmem, vmem],
        out_shape=[out, out],
        compiler_params=params(*arrays, out, out),
        cost_estimate=pl.CostEstimate(
            flops=4 * out.size, bytes_accessed=4 * bytes_of(out, out), transcendentals=0
        ),
    )(ring.places, *arrays)


def key_slots(block_section, section_parent, xref_owner, xref_block, xref_valid, first_blk):
    blocks = block_section.shape[0]
    blk_count = xref_block.shape[0]
    own = first_blk + jnp.arange(blk_count, dtype=jnp.int32)
    offsets = jnp.concatenate([jnp.array([0], jnp.int32), jnp.arange(1 - LOOK, 0, dtype=jnp.int32)])
    window = own[:, None] + offsets[None, :]
    is_block = jnp.arange(blocks, dtype=jnp.int32)

    def section_of(index):
        return jnp.sum(
            jnp.where(index[..., None] == is_block, block_section + 1, 0), axis=-1
        ) - 1

    my_sec = section_of(own)
    window_ok = section_of(window) == my_sec[:, None]
    chain = [my_sec]
    is_section = jnp.arange(section_parent.shape[0], dtype=jnp.int32)
    for _ in range(ANC - 1):
        prior = chain[-1]
        chain.append(
            jnp.sum(jnp.where(prior[:, None] == is_section, section_parent + 1, 0), axis=1) - 1
        )
    ancestors = jnp.stack(chain, axis=1)
    targets = xref_owner.reshape(blk_count, XREF) * blk_count + xref_block
    place = jnp.concatenate(
        [jnp.maximum(window, 0), blocks + jnp.maximum(ancestors, 0), targets], axis=1
    )
    valid = jnp.concatenate([window_ok, ancestors >= 0, xref_valid > 0], axis=1)
    slot = jnp.arange(SLOTS, dtype=jnp.int32)
    earlier = slot[:, None] < slot[None, :]
    before = jnp.sum(jnp.where(earlier[None], valid[:, :, None].astype(jnp.int32), 0), axis=1)
    count = jnp.sum(valid.astype(jnp.int32), axis=1)
    rank = jnp.where(valid, before, count[:, None] + slot - before)
    sorted_from = rank[:, :, None] == slot
    padded = -(-SLOTS // GROUP) * GROUP - SLOTS
    order = jnp.sum(jnp.where(sorted_from, place[:, :, None], 0), axis=1)
    is_ref = (slot >= LOOK + ANC).astype(jnp.int32)
    rounded = jnp.sum(jnp.where(sorted_from, is_ref[None, :, None], 0), axis=1)
    order, rounded = (jnp.pad(table, ((0, 0), (0, padded))) for table in (order, rounded))
    return order, rounded, count


def exchanged(block, axis, bit):
    size = lax.axis_size(axis)
    return lax.ppermute(block, axis, [(i, i ^ bit) for i in range(size)])


def exchange_order(axis):
    order, bit = [0], lax.axis_size(axis) // 2
    while bit:
        order += [index ^ bit for index in order]
        bit //= 2
    return order


def gathered_by_exchange(block, axis, after):
    parts, bit = [block], lax.axis_size(axis) // 2
    while bit:
        parts += [exchanged(part, axis, bit) for part in parts]
        bit //= 2
        if bit:
            parts = [held(part, after) for part in parts]
    return parts


def reduced_by_exchange(parts, axis, bit):
    while bit < lax.axis_size(axis):
        half = parts.shape[0] // 2
        given = exchanged(parts[half:], axis, bit)
        parts = (parts[:half].astype(jnp.float32) + given.astype(jnp.float32)).astype(jnp.bfloat16)
        bit *= 2
    return parts[0]


def held(array, after):
    return lax.optimization_barrier((array, after))[0]


def cotangent_kernel(shard_rows, order, base, me_ref, place_ref, *refs):
    out_ref, weight_ref = refs[-2:]
    parts, refs = refs[: len(order)], refs[len(order) :]
    part_width = parts[0].shape[1]
    for number, rows in enumerate(shard_rows):
        first = pl.multiple_of(place_ref[base + number], 16)
        weight_ref[pl.ds(first, rows)] = refs[number][...]
    total = None
    for part_ref, index in zip(parts, order):
        first = pl.multiple_of((me_ref[0] ^ index) * part_width, 16)
        term = product(part_ref[...], weight_ref[pl.ds(first, part_width)], 1, 0)
        total = term if total is None else total + term
    out_ref[...] = total.astype(jnp.bfloat16)


def cotangent_of_attn(parts, shards, ring, me, order, after):
    count, (tokens, part_width) = len(parts), parts[0].shape
    width = shards[0].shape[1]
    outs = [
        jax.ShapeDtypeStruct((tokens, width), jnp.bfloat16),
        jax.ShapeDtypeStruct((count * part_width, width), jnp.bfloat16),
    ]
    return pl.pallas_call(
        functools.partial(
            cotangent_kernel, [shard.shape[0] for shard in shards], order, ring.weight_places
        ),
        name="cotangent_of_attn",
        in_specs=[smem, smem] + [vmem] * (count + len(shards)) + [anywhere] * len(after),
        out_specs=[vmem, vmem],
        out_shape=outs,
        compiler_params=params(*parts, *shards, *outs),
        cost_estimate=pl.CostEstimate(
            flops=2 * count * tokens * part_width * width,
            bytes_accessed=bytes_of(*parts, *outs, *outs),
            transcendentals=0,
        ),
    )(me, ring.places, *parts, *shards, *after)


def projection_kernel(order, kv_heads, added, waits, me_ref, *refs):
    *refs, out_ref = refs
    refs = refs[waits:]
    if added:
        *refs, added_ref = refs
    part_width = out_ref.shape[2]
    weights, attns = refs[:kv_heads], refs[kv_heads:]
    blocks = len(attns) // kv_heads
    for j, index in enumerate(order):
        first = pl.multiple_of((me_ref[0] ^ index) * part_width, 16)
        for c, weight_ref in enumerate(weights):
            attn = jnp.concatenate([ref[...] for ref in attns[c * blocks : (c + 1) * blocks]], axis=0)
            term = product(attn, weight_ref[pl.ds(first, part_width)], 1, 1)
            total = term if c == 0 else total + term
        if added:
            total = total + added_ref[j].astype(jnp.float32)
        out_ref[j] = total.astype(jnp.bfloat16)


def projection_parts(attns, weights, me, order, after, added=()):
    kv_heads = len(weights)
    width, count = weights[0].shape[1], 2 * len(order)
    tokens = len(attns) // kv_heads * BLK
    part_width = weights[0].shape[0] // count
    out = jax.ShapeDtypeStruct((len(order), tokens, part_width), jnp.bfloat16)
    return pl.pallas_call(
        functools.partial(projection_kernel, order, kv_heads, bool(added), len(after)),
        name="projection_parts",
        in_specs=[smem]
        + [anywhere] * len(after)
        + [vmem] * (kv_heads + len(attns) + len(added)),
        out_specs=vmem,
        out_shape=out,
        compiler_params=params(*weights, *attns, *added, out),
        cost_estimate=pl.CostEstimate(
            flops=2 * len(order) * tokens * part_width * width * kv_heads,
            bytes_accessed=bytes_of(out, *weights, *attns),
            transcendentals=0,
        ),
    )(me, *after, *weights, *attns, *added)


def on_device(
    queries,
    keys,
    values,
    out_weight,
    d_proj,
    block_section,
    section_parent,
    xref_owner,
    xref_block,
    xref_valid,
):
    blk_count = queries.shape[0] // BLK
    kv_heads = keys.shape[1] // HEAD_DIMENSION
    width = queries.shape[1] // kv_heads
    pieces = range(blk_count)
    first_blk = lax.axis_index("seq") * blk_count
    me = lax.axis_index("head").reshape(1)

    def columns(array, index, size=HEAD_DIMENSION):
        return array[:, index * size : (index + 1) * size]

    ring = Ring("seq", keys.shape[0], out_weight.shape[1])
    section_ids = jnp.arange(section_parent.shape[0], dtype=jnp.int32)
    root_counts = jnp.sqrt(
        jnp.sum((block_section[:, None] == section_ids[None, :]).astype(jnp.float32), axis=0)
    )
    order, rounded, count = key_slots(
        block_section, section_parent, xref_owner, xref_block, xref_valid, first_blk
    )
    weight = [columns(out_weight.T, c, width) for c in range(kv_heads)]
    gather = ring.gather(
        jnp.concatenate(
            [columns(array, c) for c in range(kv_heads) for array in (keys, values)], axis=1
        )
    )
    came = gather.step()
    shards = gather.rest([order, rounded, count, root_counts, ring.places, *weight, *came])
    gathers = [ring.gather(weight[c]) for c in range(kv_heads)]
    d_parts = gathered_by_exchange(d_proj, "head", shards[-1])
    extended = extended_blocks(shards, ring.places, block_section, root_counts)
    blocks = [extended[2 * c : 2 * c + 2] for c in range(kv_heads)]

    forward = [[] for _ in range(kv_heads)]
    total = kv_heads * blk_count
    came, done = gathers[0].step(shards[-2:]), []
    steps = gathers[0].left + 1
    taken = 1
    for number in range(total):
        c, b = divmod(number, blk_count)
        ready = []
        while taken < steps and number * steps >= taken * total:
            ready = came
            came = gathers[0].step(done)
            taken += 1
        out = attention_forward(b, c, width, queries, *blocks[c], order, count, [*ready, *done])
        forward[c].append(out)
        done = [out[0]]

    parts_order = exchange_order("head")
    half = len(parts_order) // 2
    attns = [forward[c][b][0] for c in range(kv_heads) for b in pieces]
    sums_bytes = 4 * bytes_of(jax.ShapeDtypeStruct(blocks[0][0].shape, jnp.float32))
    span = 1 if sums_bytes < (30 << 20) else blk_count
    tables = (block_section, root_counts, order, count, rounded, ring.places)
    d_queries, last_arrays, weight_rows = [], [], []
    reducing = None
    for c in range(kv_heads):
        following = gathers[c + 1] if c + 1 < kv_heads else None
        if following:
            came = following.step(gathers[c].pieces[-4:-2])
            steps, taken = following.left + 1, 1
        grad, rows = cotangent_of_attn(d_parts, gathers[c].rest(), ring, me, parts_order, done)
        weight_rows.append(rows)
        done = [grad]
        sums, grad_query = [], []
        for b in range(0, blk_count, span):
            ready = []
            if following and taken < steps:
                ready = came
                came = following.step(done)
                taken += 1
            if reducing and reducing.left > 1:
                ready = [*ready, *reducing.step(done)]
            last = b + span == blk_count
            numbers = list(range(b, b + span))
            out = attention_backward(
                numbers, c, last, ring, tables, queries, grad,
                [forward[c][i] for i in numbers], *blocks[c], sums, ready,
            )
            grad_query += out[:span]
            sums = out[span : span + 2]
            done = [out[0]]
        terms, ahead, back = out[-3:]
        if reducing:
            last_arrays += [reducing.terms, *reducing.rest()]
        reducing = Reduction(ring, terms, ahead, back)
        d_queries.append(jnp.concatenate(grad_query, axis=0))

    given = projection_parts(attns, weight_rows, me, parts_order[half:], [terms])
    summed = reducing.step([given])
    kept = projection_parts(
        attns, weight_rows, me, parts_order[:half], summed, [exchanged(given, "head", 1)]
    )
    reducing.step([kept])
    last_arrays += [reducing.terms, *reducing.rest()]
    projected = reduced_by_exchange(kept, "head", 2)
    return (projected, jnp.concatenate(d_queries, axis=1), *last_sums(ring, last_arrays))


def solution(mesh):
    placed = (
        P("seq", "head"),
        P("seq", "head"),
        P("seq", "head"),
        P("head", "seq"),
        P("seq", "head"),
        P(),
        P(),
        P("seq", None),
        P("seq", None),
        P("seq", None),
    )
    return jax.shard_map(
        on_device,
        mesh=mesh,
        in_specs=placed,
        out_specs=(P("seq", "head"), P("seq", "head"), P("seq", "head"), P("seq", "head")),
        check_vma=False,
    )
```

time: 384 us -> 261 us (0.68)
  waiting for transfers between devices: 254 us -> 67.1 us
  starting transfers between devices: 3.59 us -> 52.7 us
  local copies, waits for them, and re-layouts: 3.47 us -> 16.2 us
  between operations: 13.9 us -> 1.47 us
  Pallas kernels: 101 us -> 113 us
    reduce_scatter x2 -> x0, waiting for transfers between devices: 125 us -> none  [the longest x1 90.4 us: on_device(): own_terms = lax.psum_scatter(terms, 'seq', scatter_dimension=0, tiled=True)]
    all_gather x2 -> x0, waiting for transfers between devices: 101 us -> none  [the longest x1 62.1 us: on_device(): weight = lax.all_gather(out_weight.T, 'seq', axis=0, tiled=True)]
    ppermute x0 -> x40, waiting for transfers between devices: none -> 67 us  [sent(): return lax.ppermute(block, self.axis, route)]
    ppermute x0 -> x40, starting transfers between devices: none -> 50.3 us  [sent(): return lax.ppermute(block, self.axis, route)]
    ppermute x2 -> x5, waiting for transfers between devices: 27.6 us -> 0.01 us  [exchanged(): return lax.ppermute(block, axis, [(i, i ^ bit) for i in range(size)])]
    pallas_call x4 -> x28, Pallas kernels: 101 us -> 113 us  [the longest x8 48.1 us: attention_backward(): pl.pallas_call(functools.partial(backward_kernel, numbers, head, not sums...]
    unnamed x14 -> x94, local copies, waits for them, and re-layouts: 0.04 us -> 10.7 us
  transfers between devices with their start and end apart: 6 -> 45, of which waited for: 6 -> 27; matrix products, arithmetic and copies ran while one was open for 2% -> 4% of each run, Pallas kernels for 13% -> 35%
where the time goes in v3:
time: 261 us; the launch traced here: 258 us
  Pallas kernels  113 us (43%)
  waiting for transfers between devices  67.1 us (26%)
  starting transfers between devices  52.7 us (20%)
  local copies, waits for them, and re-layouts  16.2 us (6%)
  other arithmetic  7.92 us (3%)
    ppermute x40, waiting for transfers between devices, sent(): return lax.ppermute(block, self.axis, route)  67 us
    ppermute x40, starting transfers between devices, sent(): return lax.ppermute(block, self.axis, route)  50.3 us
    pallas_call x8, Pallas kernels, attention_backward(): pl.pallas_call(functools.partial(backward_kernel, numbers, head, not sums...  48.1 us
    pallas_call x8, Pallas kernels, attention_forward(): pl.pallas_call(functools.partial(forward_kernel, block, head), name='atte...  42.2 us
    unnamed x94, local copies, waits for them, and re-layouts  10.7 us
    pallas_call x2, Pallas kernels, cotangent_of_attn(): pl.pallas_call(functools.partial(cotangent_kernel, [shard.shape[0] for sh...  9.11 us
  transfers between devices with their start and end apart: 45, of which 27 were waited for; matrix products, arithmetic and copies ran while one was open for 4% of the time, Pallas kernels for 35%

profile of v3, /device:TPU:0, one launch (start us, length us, event | category | flops | bytes accessed | tf_op | source)
XLA Modules:
  0.0 258.1 jit_solution(10002548231341878019)
XLA Ops:
  1.9 3.0 %collective-permute-start.1 = (bf16[512,512]{1,0:T(8,128)(2,1)S(1)}, bf16[512,512]{1,0:T(8,128)(2,1)S(1)}, u32[]{:S(2)}, u32[]{:S(2)}) collective-permute-start(bf16[512,512]{1,0:T(8,128)(2,1)S(1)} %pad_maximum_fusion.refs_0_), channel_id=1, source_target_pairs={{0,4},{8,0},{16,8},{24,16},{28,24},{20,28},{12,20},{4,12},{1,5},{9... | collective-permute-start | bytes 1572872 | tf_op jit(solution)/shard_map/ppermute | solution.py:350
  13.5 3.4 %collective-permute-done.1.refs_2_ = bf16[512,512]{1,0:T(8,128)(2,1)S(1)} collective-permute-done((bf16[512,512]{1,0:T(8,128)(2,1)S(1)}, bf16[512,512]{1,0:T(8,128)(2,1)S(1)}, u32[]{:S(2)}, u32[]{:S(2)}) %collective-permute-start.1) | collective-permute-done | bytes 524320 | tf_op jit(solution)/shard_map/ppermute | solution.py:350
  21.1 9.7 %collective-permute-done.2.refs_3_ = bf16[512,512]{1,0:T(8,128)(2,1)S(1)} collective-permute-done((bf16[512,512]{1,0:T(8,128)(2,1)S(1)}, bf16[512,512]{1,0:T(8,128)(2,1)S(1)}, u32[]{:S(2)}, u32[]{:S(2)}) %collective-permute-start.2) | collective-permute-done | bytes 524320 | tf_op jit(solution)/shard_map/ppermute | solution.py:350
  34.1 9.6 %collective-permute-done.4.refs_5_ = bf16[512,512]{1,0:T(8,128)(2,1)S(1)} collective-permute-done((bf16[512,512]{1,0:T(8,128)(2,1)S(1)}, bf16[512,512]{1,0:T(8,128)(2,1)S(1)}, u32[]{:S(2)}, u32[]{:S(2)}) %collective-permute-start.4) | collective-permute-done | bytes 524320 | tf_op jit(solution)/shard_map/ppermute | solution.py:350
  47.0 5.1 %collective-permute-done.10.refs_7_ = bf16[256,512]{1,0:T(8,128)(2,1)S(1)} collective-permute-done((bf16[256,512]{1,0:T(8,128)(2,1)S(1)}, bf16[256,512]{1,0:T(8,128)(2,1)S(1)}, u32[]{:S(2)}, u32[]{:S(2)}) %collective-permute-start.10) | collective-permute-done | bytes 262176 | tf_op jit(solution)/shard_map/ppermute | solution.py:350
  59.5 2.9 %extended_blocks.1 = (bf16[4608,128]{1,0:T(8,128)(2,1)S(1)}, bf16[4608,128]{1,0:T(8,128)(2,1)S(1)}, bf16[4608,128]{1,0:T(8,128)(2,1)S(1)}, bf16[4608,128]{1,0:T(8,128)(2,1)S(1)}) custom-call(s32[32]{0:T(128)S(1)} %copy-done.36, f32[4]{0:T(128)S(1)} %copy-done.38, s32[26]{0:T(128)S(1)} %dynamic-slice_bitcast_fusion.place_ref, ...), custom_call_target="tpu_custom_call" | custom-call | flops 4718592 | bytes 14155776 | tf_op jit(solution)/shard_map/extended_blocks/pallas_call | solution.py:244
  62.4 4.9 %attention_forward.8 = (bf16[128,640]{1,0:T(8,128)(2,1)S(1)}, f32[640,128]{1,0:T(8,128)S(1)}) custom-call(s32[4,18]{1,0:T(4,128)S(1)} %get-tuple-element.181.order_ref, s32[4]{0:T(128)S(1)} %get-tuple-element.182.count_ref, bf16[512,1280]{1,0:T(8,128)(2,1)S(1)} %copy-done, bf16[4608,128]{1,0:T(8,128)(2,1)S(1)} %get-tuple-element.102.keys_ref, ...), custom_call_target="tpu_custom_call" | custom-call | flops 754974720 | bytes 4194304 | tf_op jit(solution)/shard_map/attention_forward/pallas_call | solution.py:266
  67.3 4.9 %attention_forward.9 = (bf16[128,640]{1,0:T(8,128)(2,1)S(1)}, f32[640,128]{1,0:T(8,128)S(1)}) custom-call(s32[4,18]{1,0:T(4,128)S(1)} %get-tuple-element.181.order_ref, s32[4]{0:T(128)S(1)} %get-tuple-element.182.count_ref, bf16[512,1280]{1,0:T(8,128)(2,1)S(1)} %copy-done, bf16[4608,128]{1,0:T(8,128)(2,1)S(1)} %get-tuple-element.102.keys_ref, ...), custom_call_target="tpu_custom_call" | custom-call | flops 754974720 | bytes 4194304 | tf_op jit(solution)/shard_map/attention_forward/pallas_call | solution.py:266
  73.0 3.6 %collective-permute-start.13 = (bf16[320,640]{1,0:T(8,128)(2,1)S(1)}, bf16[320,640]{1,0:T(8,128)(2,1)S(1)}, u32[]{:S(2)}, u32[]{:S(2)}) collective-permute-start(bf16[320,640]{1,0:T(8,128)(2,1)S(1)} %collective-permute-done.11.refs_0_.refs_5_), channel_id=1, source_target_pairs={{0,8},{8,16},{16,24},{24,28},{28,20},{20,12},{12,4},{4,0},{1,9},{9... | collective-permute-start | bytes 1228808 | tf_op jit(solution)/shard_map/ppermute | solution.py:350
  76.7 4.9 %attention_forward.10 = (bf16[128,640]{1,0:T(8,128)(2,1)S(1)}, f32[640,128]{1,0:T(8,128)S(1)}) custom-call(s32[4,18]{1,0:T(4,128)S(1)} %get-tuple-element.181.order_ref, s32[4]{0:T(128)S(1)} %get-tuple-element.182.count_ref, bf16[512,1280]{1,0:T(8,128)(2,1)S(1)} %copy-done, bf16[4608,128]{1,0:T(8,128)(2,1)S(1)} %get-tuple-element.102.keys_ref, ...), custom_call_target="tpu_custom_call" | custom-call | flops 754974720 | bytes 4194304 | tf_op jit(solution)/shard_map/attention_forward/pallas_call | solution.py:266
  82.4 6.3 %attention_forward.11 = (bf16[128,640]{1,0:T(8,128)(2,1)S(1)}, f32[640,128]{1,0:T(8,128)S(1)}) custom-call(s32[4,18]{1,0:T(4,128)S(1)} %get-tuple-element.181.order_ref, s32[4]{0:T(128)S(1)} %get-tuple-element.182.count_ref, bf16[512,1280]{1,0:T(8,128)(2,1)S(1)} %copy-done, bf16[4608,128]{1,0:T(8,128)(2,1)S(1)} %get-tuple-element.102.keys_ref, ...), custom_call_target="tpu_custom_call" | custom-call | flops 754974720 | bytes 4194304 | tf_op jit(solution)/shard_map/attention_forward/pallas_call | solution.py:266
  89.4 4.6 %collective-permute-start.15 = (bf16[320,640]{1,0:T(8,128)(2,1)S(1)}, bf16[320,640]{1,0:T(8,128)(2,1)S(1)}, u32[]{:S(2)}, u32[]{:S(2)}) collective-permute-start(bf16[320,640]{1,0:T(8,128)(2,1)S(1)} %collective-permute-done.13.refs_0_.refs_7_), channel_id=1, source_target_pairs={{0,8},{8,16},{16,24},{24,28},{28,20},{20,12},{12,4},{4,0},{1,9},{9... | collective-permute-start | bytes 1228808 | tf_op jit(solution)/shard_map/ppermute | solution.py:350
  94.3 4.9 %attention_forward.12 = (bf16[128,640]{1,0:T(8,128)(2,1)S(1)}, f32[640,128]{1,0:T(8,128)S(1)}) custom-call(s32[4,18]{1,0:T(4,128)S(1)} %get-tuple-element.181.order_ref, s32[4]{0:T(128)S(1)} %get-tuple-element.182.count_ref, bf16[512,1280]{1,0:T(8,128)(2,1)S(1)} %copy-done, bf16[4608,128]{1,0:T(8,128)(2,1)S(1)} %get-tuple-element.114.keys_ref, ...), custom_call_target="tpu_custom_call" | custom-call | flops 754974720 | bytes 4194304 | tf_op jit(solution)/shard_map/attention_forward/pallas_call | solution.py:266
  99.2 4.3 %collective-permute-done.15.refs_0_.refs_9_ = bf16[320,640]{1,0:T(8,128)(2,1)S(1)} collective-permute-done((bf16[320,640]{1,0:T(8,128)(2,1)S(1)}, bf16[320,640]{1,0:T(8,128)(2,1)S(1)}, u32[]{:S(2)}, u32[]{:S(2)}) %collective-permute-start.15) | collective-permute-done | bytes 409632 | tf_op jit(solution)/shard_map/ppermute | solution.py:350
  107.7 4.9 %attention_forward.13 = (bf16[128,640]{1,0:T(8,128)(2,1)S(1)}, f32[640,128]{1,0:T(8,128)S(1)}) custom-call(s32[4,18]{1,0:T(4,128)S(1)} %get-tuple-element.181.order_ref, s32[4]{0:T(128)S(1)} %get-tuple-element.182.count_ref, bf16[512,1280]{1,0:T(8,128)(2,1)S(1)} %copy-done, bf16[4608,128]{1,0:T(8,128)(2,1)S(1)} %get-tuple-element.114.keys_ref, ...), custom_call_target="tpu_custom_call" | custom-call | flops 754974720 | bytes 4194304 | tf_op jit(solution)/shard_map/attention_forward/pallas_call | solution.py:266
  120.3 4.9 %attention_forward.14 = (bf16[128,640]{1,0:T(8,128)(2,1)S(1)}, f32[640,128]{1,0:T(8,128)S(1)}) custom-call(s32[4,18]{1,0:T(4,128)S(1)} %get-tuple-element.181.order_ref, s32[4]{0:T(128)S(1)} %get-tuple-element.182.count_ref, bf16[512,1280]{1,0:T(8,128)(2,1)S(1)} %copy-done, bf16[4608,128]{1,0:T(8,128)(2,1)S(1)} %get-tuple-element.114.keys_ref, ...), custom_call_target="tpu_custom_call" | custom-call | flops 754974720 | bytes 4194304 | tf_op jit(solution)/shard_map/attention_forward/pallas_call | solution.py:266
  125.3 6.4 %attention_forward.15 = (bf16[128,640]{1,0:T(8,128)(2,1)S(1)}, f32[640,128]{1,0:T(8,128)S(1)}) custom-call(s32[4,18]{1,0:T(4,128)S(1)} %get-tuple-element.181.order_ref, s32[4]{0:T(128)S(1)} %get-tuple-element.182.count_ref, bf16[512,1280]{1,0:T(8,128)(2,1)S(1)} %copy-done, bf16[4608,128]{1,0:T(8,128)(2,1)S(1)} %get-tuple-element.114.keys_ref, ...), custom_call_target="tpu_custom_call" | custom-call | flops 754974720 | bytes 4194304 | tf_op jit(solution)/shard_map/attention_forward/pallas_call | solution.py:266
  131.9 4.5 %cotangent_of_attn.2 = (bf16[512,640]{1,0:T(8,128)(2,1)S(1)}, bf16[2560,640]{1,0:T(8,128)(2,1)S(1)}) custom-call(s32[1]{0:T(128)} %bitcast.me_ref, s32[26]{0:T(128)S(1)} %dynamic-slice_bitcast_fusion.place_ref, bf16[512,640]{1,0:T(8,128)(2,1)} %refs_0_.1, bf16[512,640]{1,0:T(8,128)(2,1)} %collective-permute-done.7.refs_1_, bf16[512,640]{1,0:T(8,128)(2,1)S(1)} %copy-done.41, ...), custom_call_target="tpu_custom_call" | custom-call | flops 1677721600 | bytes 10485760 | tf_op jit(solution)/shard_map/cotangent_of_attn/pallas_call | solution.py:556
  136.5 3.4 %collective-permute-start.21 = (bf16[320,640]{1,0:T(8,128)(2,1)}, bf16[320,640]{1,0:T(8,128)(2,1)S(1)}, u32[]{:S(2)}, u32[]{:S(2)}) collective-permute-start(bf16[320,640]{1,0:T(8,128)(2,1)} %collective-permute-done.17.refs_2_.refs_5_), channel_id=1, source_target_pairs={{0,8},{8,16},{16,24},{24,28},{28,20},{20,12},{12,4},{4,0},{1,9},{9... | collective-permute-start | bytes 1228808 | tf_op jit(solution)/shard_map/ppermute | solution.py:350
  139.9 5.6 %attention_backward.8 = (bf16[128,640]{1,0:T(8,128)(2,1)S(1)}, f32[4608,128]{1,0:T(8,128)S(1)}, f32[4608,128]{1,0:T(8,128)S(1)}) custom-call(s32[32]{0:T(128)S(1)} %copy-done.37, f32[4]{0:T(128)S(1)} %copy-done.39, s32[4,18]{1,0:T(4,128)S(1)} %get-tuple-element.181.order_ref, s32[4]{0:T(128)S(1)} %get-tuple-element.182.count_ref, ...), custom_call_target="tpu_custom_call" | custom-call | flops 1887436800 | bytes 4194304 | tf_op jit(solution)/shard_map/attention_backward/pallas_call | solution.py:299
  151.5 5.3 %attention_backward.9 = (bf16[128,640]{1,0:T(8,128)(2,1)S(1)}, f32[4608,128]{1,0:T(8,128)S(1)}, f32[4608,128]{1,0:T(8,128)S(1)}) custom-call(s32[32]{0:T(128)S(1)} %copy-done.37, f32[4]{0:T(128)S(1)} %copy-done.39, s32[4,18]{1,0:T(4,128)S(1)} %get-tuple-element.181.order_ref, ...), custom_call_target="tpu_custom_call", output_to_operand_aliasing={{1}: (14, {}), {2}: (15, {})} | custom-call | flops 1887436800 | bytes 4194304 | tf_op jit(solution)/shard_map/attention_backward/pallas_call | solution.py:299
  161.7 5.3 %attention_backward.10 = (bf16[128,640]{1,0:T(8,128)(2,1)S(1)}, f32[4608,128]{1,0:T(8,128)S(1)}, f32[4608,128]{1,0:T(8,128)S(1)}) custom-call(s32[32]{0:T(128)S(1)} %copy-done.37, f32[4]{0:T(128)S(1)} %copy-done.39, s32[4,18]{1,0:T(4,128)S(1)} %get-tuple-element.181.order_ref, ...), custom_call_target="tpu_custom_call", output_to_operand_aliasing={{1}: (14, {}), {2}: (15, {})} | custom-call | flops 1887436800 | bytes 4194304 | tf_op jit(solution)/shard_map/attention_backward/pallas_call | solution.py:299
  167.0 7.7 %attention_backward.11 = (bf16[128,640]{1,0:T(8,128)(2,1)S(1)}, f32[4608,128]{1,0:T(8,128)S(1)}, f32[4608,128]{1,0:T(8,128)S(1)}, bf16[4096,256]{1,0:T(8,128)(2,...) custom-call(s32[32]{0:T(128)S(1)} %copy-done.37, ...), custom_call_target="tpu_custom_call", output_to_operand_aliasing={{1}: (12, {}), {2}: (13, {})} | custom-call | flops 1887436800 | bytes 4194304 | tf_op jit(solution)/shard_map/attention_backward/pallas_call | solution.py:299
  176.8 4.6 %cotangent_of_attn.3 = (bf16[512,640]{1,0:T(8,128)(2,1)S(1)}, bf16[2560,640]{1,0:T(8,128)(2,1)S(1)}) custom-call(s32[1]{0:T(128)} %bitcast.me_ref, s32[26]{0:T(128)S(1)} %dynamic-slice_bitcast_fusion.place_ref, bf16[512,640]{1,0:T(8,128)(2,1)} %refs_0_.1, bf16[512,640]{1,0:T(8,128)(2,1)} %collective-permute-done.7.refs_1_, bf16[512,640]{1,0:T(8,128)(2,1)S(1)} %copy-done.41, ...), custom_call_target="tpu_custom_call" | custom-call | flops 1677721600 | bytes 10485760 | tf_op jit(solution)/shard_map/cotangent_of_attn/pallas_call | solution.py:556
  185.8 5.6 %attention_backward.12 = (bf16[128,640]{1,0:T(8,128)(2,1)S(1)}, f32[4608,128]{1,0:T(8,128)S(1)}, f32[4608,128]{1,0:T(8,128)S(1)}) custom-call(s32[32]{0:T(128)S(1)} %copy-done.37, f32[4]{0:T(128)S(1)} %copy-done.39, s32[4,18]{1,0:T(4,128)S(1)} %get-tuple-element.181.order_ref, s32[4]{0:T(128)S(1)} %get-tuple-element.182.count_ref, ...), custom_call_target="tpu_custom_call" | custom-call | flops 1887436800 | bytes 4194304 | tf_op jit(solution)/shard_map/attention_backward/pallas_call | solution.py:299
  192.6 5.4 %attention_backward.13 = (bf16[128,640]{1,0:T(8,128)(2,1)S(1)}, f32[4608,128]{1,0:T(8,128)S(1)}, f32[4608,128]{1,0:T(8,128)S(1)}) custom-call(s32[32]{0:T(128)S(1)} %copy-done.37, f32[4]{0:T(128)S(1)} %copy-done.39, s32[4,18]{1,0:T(4,128)S(1)} %get-tuple-element.181.order_ref, ...), custom_call_target="tpu_custom_call", output_to_operand_aliasing={{1}: (14, {}), {2}: (15, {})} | custom-call | flops 1887436800 | bytes 4194304 | tf_op jit(solution)/shard_map/attention_backward/pallas_call | solution.py:299
  198.0 5.6 %attention_backward.14 = (bf16[128,640]{1,0:T(8,128)(2,1)S(1)}, f32[4608,128]{1,0:T(8,128)S(1)}, f32[4608,128]{1,0:T(8,128)S(1)}) custom-call(s32[32]{0:T(128)S(1)} %copy-done.37, f32[4]{0:T(128)S(1)} %copy-done.39, s32[4,18]{1,0:T(4,128)S(1)} %get-tuple-element.181.order_ref, ...), custom_call_target="tpu_custom_call", output_to_operand_aliasing={{1}: (12, {}), {2}: (13, {})} | custom-call | flops 1887436800 | bytes 4194304 | tf_op jit(solution)/shard_map/attention_backward/pallas_call | solution.py:299
  203.6 7.8 %attention_backward.15 = (bf16[128,640]{1,0:T(8,128)(2,1)S(1)}, f32[4608,128]{1,0:T(8,128)S(1)}, f32[4608,128]{1,0:T(8,128)S(1)}, bf16[4096,256]{1,0:T(8,128)(2,...) custom-call(s32[32]{0:T(128)S(1)} %copy-done.37, ...), custom_call_target="tpu_custom_call", output_to_operand_aliasing={{1}: (12, {}), {2}: (13, {})} | custom-call | flops 1887436800 | bytes 4194304 | tf_op jit(solution)/shard_map/attention_backward/pallas_call | solution.py:299
  214.0 4.6 %collective-permute-start.31 = (bf16[256,256]{1,0:T(8,128)(2,1)S(1)}, bf16[256,256]{1,0:T(8,128)(2,1)S(1)}, u32[]{:S(2)}, u32[]{:S(2)}) collective-permute-start(bf16[256,256]{1,0:T(8,128)(2,1)S(1)} %get-tuple-element.162), channel_id=1, source_target_pairs={{0,8},{8,16},{16,24},{24,28},{28,20},{20,12},{12,4},{4,0},{1,9},{9... | collective-permute-start | bytes 393224 | tf_op jit(solution)/shard_map/ppermute | solution.py:350
  218.6 3.4 %collective-permute-done.31.ahead_in = bf16[256,256]{1,0:T(8,128)(2,1)S(1)} collective-permute-done((bf16[256,256]{1,0:T(8,128)(2,1)S(1)}, bf16[256,256]{1,0:T(8,128)(2,1)S(1)}, u32[]{:S(2)}, u32[]{:S(2)}) %collective-permute-start.31) | collective-permute-done | bytes 131104 | tf_op jit(solution)/shard_map/ppermute | solution.py:350
  226.8 2.5 projection_parts.3.refs_0_
  251.4 3.4 %collective-permute-done.43.refs_4_ = bf16[512,256]{1,0:T(8,128)(2,1)S(1)} collective-permute-done((bf16[512,256]{1,0:T(8,128)(2,1)S(1)}, bf16[512,256]{1,0:T(8,128)(2,1)S(1)}, u32[]{:S(2)}, u32[]{:S(2)}) %collective-permute-start.43) | collective-permute-done | bytes 262176 | tf_op jit(solution)/shard_map/ppermute | solution.py:350
  (225 shorter events, 93.7 us)
Async XLA Ops:
  1.9 15.0 %collective-permute-start.1 = (bf16[512,512]{1,0:T(8,128)(2,1)S(1)}, bf16[512,512]{1,0:T(8,128)(2,1)S(1)}, u32[]{:S(2)}, u32[]{:S(2)}) collective-permute-start(bf16[512,512]{1,0:T(8,128)(2,1)S(1)} %pad_maximum_fusion.refs_0_), channel_id=1, source_target_pairs={{0,4},{8,0},{16,8},{24,16},{28,24},{20,28},{12,20},{4,12},{1,5},{9... | collective-permute-start | bytes 1572872 | tf_op jit(solution)/shard_map/ppermute | solution.py:350
  4.9 13.4 %collective-permute-start = (bf16[512,512]{1,0:T(8,128)(2,1)S(1)}, bf16[512,512]{1,0:T(8,128)(2,1)S(1)}, u32[]{:S(2)}, u32[]{:S(2)}) collective-permute-start(bf16[512,512]{1,0:T(8,128)(2,1)S(1)} %pad_maximum_fusion.refs_0_), channel_id=1, source_target_pairs={{0,8},{8,16},{16,24},{24,28},{28,20},{20,12},{12,4},{4,0},{1,9},{9... | collective-permute-start | bytes 1572872 | tf_op jit(solution)/shard_map/ppermute | solution.py:350
  18.3 12.5 %collective-permute-start.2 = (bf16[512,512]{1,0:T(8,128)(2,1)S(1)}, bf16[512,512]{1,0:T(8,128)(2,1)S(1)}, u32[]{:S(2)}, u32[]{:S(2)}) collective-permute-start(bf16[512,512]{1,0:T(8,128)(2,1)S(1)} %collective-permute-done.refs_1_), channel_id=1, source_target_pairs={{0,8},{8,16},{16,24},{24,28},{28,20},{20,12},{12,4},{4,0},{1,9},{9... | collective-permute-start | bytes 1572872 | tf_op jit(solution)/shard_map/ppermute | solution.py:350
  19.5 12.5 %collective-permute-start.3 = (bf16[512,512]{1,0:T(8,128)(2,1)S(1)}, bf16[512,512]{1,0:T(8,128)(2,1)S(1)}, u32[]{:S(2)}, u32[]{:S(2)}) collective-permute-start(bf16[512,512]{1,0:T(8,128)(2,1)S(1)} %collective-permute-done.1.refs_2_), channel_id=1, source_target_pairs={{0,4},{8,0},{16,8},{24,16},{28,24},{20,28},{12,20},{4,12},{1,5},{9... | collective-permute-start | bytes 1572872 | tf_op jit(solution)/shard_map/ppermute | solution.py:350
  32.1 11.7 %collective-permute-start.4 = (bf16[512,512]{1,0:T(8,128)(2,1)S(1)}, bf16[512,512]{1,0:T(8,128)(2,1)S(1)}, u32[]{:S(2)}, u32[]{:S(2)}) collective-permute-start(bf16[512,512]{1,0:T(8,128)(2,1)S(1)} %collective-permute-done.2.refs_3_), channel_id=1, source_target_pairs={{0,8},{8,16},{16,24},{24,28},{28,20},{20,12},{12,4},{4,0},{1,9},{9... | collective-permute-start | bytes 1572872 | tf_op jit(solution)/shard_map/ppermute | solution.py:350
  33.6 11.2 %collective-permute-start.5 = (bf16[512,512]{1,0:T(8,128)(2,1)S(1)}, bf16[512,512]{1,0:T(8,128)(2,1)S(1)}, u32[]{:S(2)}, u32[]{:S(2)}) collective-permute-start(bf16[512,512]{1,0:T(8,128)(2,1)S(1)} %collective-permute-done.3.refs_4_), channel_id=1, source_target_pairs={{0,4},{8,0},{16,8},{24,16},{28,24},{20,28},{12,20},{4,12},{1,5},{9... | collective-permute-start | bytes 1572872 | tf_op jit(solution)/shard_map/ppermute | solution.py:350
  54.1 18.9 %collective-permute-start.11 = (bf16[320,640]{1,0:T(8,128)(2,1)S(1)}, bf16[320,640]{1,0:T(8,128)(2,1)S(1)}, u32[]{:S(2)}, u32[]{:S(2)}) collective-permute-start(bf16[320,640]{1,0:T(8,128)(2,1)S(1)} %get-tuple-element.101.refs_4_), channel_id=1, source_target_pairs={{0,8},{8,16},{16,24},{24,28},{28,20},{20,12},{12,4},{4,0},{1,9},{9... | collective-permute-start | bytes 1228808 | tf_op jit(solution)/shard_map/ppermute | solution.py:350
  55.5 17.4 %collective-permute-start.12 = (bf16[320,640]{1,0:T(8,128)(2,1)S(1)}, bf16[320,640]{1,0:T(8,128)(2,1)S(1)}, u32[]{:S(2)}, u32[]{:S(2)}) collective-permute-start(bf16[320,640]{1,0:T(8,128)(2,1)S(1)} %get-tuple-element.101.refs_4_), channel_id=1, source_target_pairs={{0,4},{8,0},{16,8},{24,16},{28,24},{20,28},{12,20},{4,12},{1,5},{9... | collective-permute-start | bytes 1228808 | tf_op jit(solution)/shard_map/ppermute | solution.py:350
  56.9 37.1 %collective-permute-start.7 = (bf16[512,640]{1,0:T(8,128)(2,1)}, bf16[512,640]{1,0:T(8,128)(2,1)}, u32[]{:S(2)}, u32[]{:S(2)}) collective-permute-start(bf16[512,640]{1,0:T(8,128)(2,1)} %refs_0_.1), channel_id=1, source_target_pairs={{0,2},{1,3},{2,0},{3,1},{4,6},{5,7},{6,4},{7,5},{8,10},{9,11},{10,... | collective-permute-start | bytes 1966088 | tf_op jit(solution)/shard_map/ppermute | solution.py:500
  73.0 16.4 %collective-permute-start.13 = (bf16[320,640]{1,0:T(8,128)(2,1)S(1)}, bf16[320,640]{1,0:T(8,128)(2,1)S(1)}, u32[]{:S(2)}, u32[]{:S(2)}) collective-permute-start(bf16[320,640]{1,0:T(8,128)(2,1)S(1)} %collective-permute-done.11.refs_0_.refs_5_), channel_id=1, source_target_pairs={{0,8},{8,16},{16,24},{24,28},{28,20},{20,12},{12,4},{4,0},{1,9},{9... | collective-permute-start | bytes 1228808 | tf_op jit(solution)/shard_map/ppermute | solution.py:350
  76.7 12.7 %collective-permute-start.14 = (bf16[320,640]{1,0:T(8,128)(2,1)S(1)}, bf16[320,640]{1,0:T(8,128)(2,1)S(1)}, u32[]{:S(2)}, u32[]{:S(2)}) collective-permute-start(bf16[320,640]{1,0:T(8,128)(2,1)S(1)} %collective-permute-done.12.refs_1_.refs_6_), channel_id=1, source_target_pairs={{0,4},{8,0},{16,8},{24,16},{28,24},{20,28},{12,20},{4,12},{1,5},{9... | collective-permute-start | bytes 1228808 | tf_op jit(solution)/shard_map/ppermute | solution.py:350
  76.7 37.8 %collective-permute-start.8 = (bf16[512,640]{1,0:T(8,128)(2,1)}, bf16[512,640]{1,0:T(8,128)(2,1)S(1)}, u32[]{:S(2)}, u32[]{:S(2)}) collective-permute-start(bf16[512,640]{1,0:T(8,128)(2,1)} %refs_0_.1), channel_id=1, source_target_pairs={{0,1},{1,0},{2,3},{3,2},{4,5},{5,4},{6,7},{7,6},{8,9},{9,8},{10,11... | collective-permute-start | bytes 1966088 | tf_op jit(solution)/shard_map/ppermute | solution.py:500
  89.4 14.1 %collective-permute-start.15 = (bf16[320,640]{1,0:T(8,128)(2,1)S(1)}, bf16[320,640]{1,0:T(8,128)(2,1)S(1)}, u32[]{:S(2)}, u32[]{:S(2)}) collective-permute-start(bf16[320,640]{1,0:T(8,128)(2,1)S(1)} %collective-permute-done.13.refs_0_.refs_7_), channel_id=1, source_target_pairs={{0,8},{8,16},{16,24},{24,28},{28,20},{20,12},{12,4},{4,0},{1,9},{9... | collective-permute-start | bytes 1228808 | tf_op jit(solution)/shard_map/ppermute | solution.py:350
  94.1 11.6 %collective-permute-start.16 = (bf16[320,640]{1,0:T(8,128)(2,1)S(1)}, bf16[320,640]{1,0:T(8,128)(2,1)S(1)}, u32[]{:S(2)}, u32[]{:S(2)}) collective-permute-start(bf16[320,640]{1,0:T(8,128)(2,1)S(1)} %collective-permute-done.14.refs_1_.refs_8_), channel_id=1, source_target_pairs={{0,4},{8,0},{16,8},{24,16},{28,24},{20,28},{12,20},{4,12},{1,5},{9... | collective-permute-start | bytes 1228808 | tf_op jit(solution)/shard_map/ppermute | solution.py:350
  94.1 37.7 %collective-permute-start.9 = (bf16[512,640]{1,0:T(8,128)(2,1)}, bf16[512,640]{1,0:T(8,128)(2,1)}, u32[]{:S(2)}, u32[]{:S(2)}) collective-permute-start(bf16[512,640]{1,0:T(8,128)(2,1)} %collective-permute-done.7.refs_1_), channel_id=1, source_target_pairs={{0,1},{1,0},{2,3},{3,2},{4,5},{5,4},{6,7},{7,6},{8,9},{9,8},{10,11... | collective-permute-start | bytes 1966088 | tf_op jit(solution)/shard_map/ppermute | solution.py:500
  105.7 30.8 %collective-permute-start.17 = (bf16[320,640]{1,0:T(8,128)(2,1)}, bf16[320,640]{1,0:T(8,128)(2,1)}, u32[]{:S(2)}, u32[]{:S(2)}) collective-permute-start(bf16[320,640]{1,0:T(8,128)(2,1)} %get-tuple-element.113.refs_4_), channel_id=1, source_target_pairs={{0,8},{8,16},{16,24},{24,28},{28,20},{20,12},{12,4},{4,0},{1,9},{9... | collective-permute-start | bytes 1228808 | tf_op jit(solution)/shard_map/ppermute | solution.py:350
  107.0 29.4 %collective-permute-start.18 = (bf16[320,640]{1,0:T(8,128)(2,1)}, bf16[320,640]{1,0:T(8,128)(2,1)}, u32[]{:S(2)}, u32[]{:S(2)}) collective-permute-start(bf16[320,640]{1,0:T(8,128)(2,1)} %get-tuple-element.113.refs_4_), channel_id=1, source_target_pairs={{0,4},{8,0},{16,8},{24,16},{28,24},{20,28},{12,20},{4,12},{1,5},{9... | collective-permute-start | bytes 1228808 | tf_op jit(solution)/shard_map/ppermute | solution.py:350
  114.2 17.6 %collective-permute-start.20 = (bf16[160,640]{1,0:T(8,128)(2,1)}, bf16[160,640]{1,0:T(8,128)(2,1)}, u32[]{:S(2)}, u32[]{:S(2)}) collective-permute-start(bf16[160,640]{1,0:T(8,128)(2,1)} %slice.51), channel_id=1, source_target_pairs={{0,4},{8,0},{16,8},{24,16},{28,24},{20,28},{12,20},{4,12},{1,5},{9... | collective-permute-start | bytes 614408 | tf_op jit(solution)/shard_map/ppermute | solution.py:350
  115.3 16.5 %collective-permute-start.19 = (bf16[160,640]{1,0:T(8,128)(2,1)}, bf16[160,640]{1,0:T(8,128)(2,1)}, u32[]{:S(2)}, u32[]{:S(2)}) collective-permute-start(bf16[160,640]{1,0:T(8,128)(2,1)} %slice.50), channel_id=1, source_target_pairs={{0,8},{8,16},{16,24},{24,28},{28,20},{20,12},{12,4},{4,0},{1,9},{9... | collective-permute-start | bytes 614408 | tf_op jit(solution)/shard_map/ppermute | solution.py:350
  136.5 10.9 %collective-permute-start.21 = (bf16[320,640]{1,0:T(8,128)(2,1)}, bf16[320,640]{1,0:T(8,128)(2,1)S(1)}, u32[]{:S(2)}, u32[]{:S(2)}) collective-permute-start(bf16[320,640]{1,0:T(8,128)(2,1)} %collective-permute-done.17.refs_2_.refs_5_), channel_id=1, source_target_pairs={{0,8},{8,16},{16,24},{24,28},{28,20},{20,12},{12,4},{4,0},{1,9},{9... | collective-permute-start | bytes 1228808 | tf_op jit(solution)/shard_map/ppermute | solution.py:350
  139.9 9.6 %collective-permute-start.22 = (bf16[320,640]{1,0:T(8,128)(2,1)}, bf16[320,640]{1,0:T(8,128)(2,1)S(1)}, u32[]{:S(2)}, u32[]{:S(2)}) collective-permute-start(bf16[320,640]{1,0:T(8,128)(2,1)} %collective-permute-done.18.refs_3_.refs_6_), channel_id=1, source_target_pairs={{0,4},{8,0},{16,8},{24,16},{28,24},{20,28},{12,20},{4,12},{1,5},{9... | collective-permute-start | bytes 1228808 | tf_op jit(solution)/shard_map/ppermute | solution.py:350
  150.0 9.5 %collective-permute-start.24 = (bf16[320,640]{1,0:T(8,128)(2,1)S(1)}, bf16[320,640]{1,0:T(8,128)(2,1)S(1)}, u32[]{:S(2)}, u32[]{:S(2)}) collective-permute-start(bf16[320,640]{1,0:T(8,128)(2,1)S(1)} %collective-permute-done.22.refs_3_.refs_8_), channel_id=1, source_target_pairs={{0,4},{8,0},{16,8},{24,16},{28,24},{20,28},{12,20},{4,12},{1,5},{9... | collective-permute-start | bytes 1228808 | tf_op jit(solution)/shard_map/ppermute | solution.py:350
  159.6 17.2 %collective-permute-start.26 = (bf16[160,640]{1,0:T(8,128)(2,1)S(1)}, bf16[160,640]{1,0:T(8,128)(2,1)S(1)}, u32[]{:S(2)}, u32[]{:S(2)}) collective-permute-start(bf16[160,640]{1,0:T(8,128)(2,1)S(1)} %slice.53), channel_id=1, source_target_pairs={{0,4},{8,0},{16,8},{24,16},{28,24},{20,28},{12,20},{4,12},{1,5},{9... | collective-permute-start | bytes 614408 | tf_op jit(solution)/shard_map/ppermute | solution.py:350
  161.1 15.7 %collective-permute-start.25 = (bf16[160,640]{1,0:T(8,128)(2,1)S(1)}, bf16[160,640]{1,0:T(8,128)(2,1)S(1)}, u32[]{:S(2)}, u32[]{:S(2)}) collective-permute-start(bf16[160,640]{1,0:T(8,128)(2,1)S(1)} %slice.52), channel_id=1, source_target_pairs={{0,8},{8,16},{16,24},{24,28},{28,20},{20,12},{12,4},{4,0},{1,9},{9... | collective-permute-start | bytes 614408 | tf_op jit(solution)/shard_map/ppermute | solution.py:350
  213.9 12.9 %collective-permute-start.33 = (bf16[2,512,640]{2,1,0:T(8,128)(2,1)S(1)}, bf16[2,512,640]{2,1,0:T(8,128)(2,1)S(1)}, u32[]{:S(2)}, u32[]{:S(2)}) collective-permute-start(bf16[2,512,640]{2,1,0:T(8,128)(2,1)S(1)} %projection_parts.2.refs_0_), channel_id=1, source_target_pairs={{0,1},{1,0},{2,3},{3,2},{4,5},{5,4},{6,7},{7,6},{8,9},{9,8},{10,11... | collective-permute-start | bytes 3932168 | tf_op jit(solution)/shard_map/ppermute | solution.py:500
  229.4 27.7 %collective-permute-start.34 = (bf16[1,512,640]{2,1,0:T(8,128)(2,1)S(1)}, bf16[1,512,640]{2,1,0:T(8,128)(2,1)S(1)}, u32[]{:S(2)}, u32[]{:S(2)}) collective-permute-start(bf16[1,512,640]{2,1,0:T(8,128)(2,1)S(1)} %slice.59), channel_id=1, source_target_pairs={{0,2},{1,3},{2,0},{3,1},{4,6},{5,7},{6,4},{7,5},{8,10},{9,11},{10,... | collective-permute-start | bytes 1966088 | tf_op jit(solution)/shard_map/ppermute | solution.py:500
  230.1 9.2 %collective-permute-start.35 = (bf16[512,256]{1,0:T(8,128)(2,1)S(1)}, bf16[512,256]{1,0:T(8,128)(2,1)S(1)}, u32[]{:S(2)}, u32[]{:S(2)}) collective-permute-start(bf16[512,256]{1,0:T(8,128)(2,1)S(1)} %get-tuple-element.153.refs_2_), channel_id=1, source_target_pairs={{0,8},{8,16},{16,24},{24,28},{28,20},{20,12},{12,4},{4,0},{1,9},{9... | collective-permute-start | bytes 786440 | tf_op jit(solution)/shard_map/ppermute | solution.py:350
  230.9 9.3 %collective-permute-start.36 = (bf16[512,256]{1,0:T(8,128)(2,1)S(1)}, bf16[512,256]{1,0:T(8,128)(2,1)S(1)}, u32[]{:S(2)}, u32[]{:S(2)}) collective-permute-start(bf16[512,256]{1,0:T(8,128)(2,1)S(1)} %get-tuple-element.154.refs_3_), channel_id=1, source_target_pairs={{0,4},{8,0},{16,8},{24,16},{28,24},{20,28},{12,20},{4,12},{1,5},{9... | collective-permute-start | bytes 786440 | tf_op jit(solution)/shard_map/ppermute | solution.py:350
  235.2 9.7 %collective-permute-start.41 = (bf16[512,256]{1,0:T(8,128)(2,1)S(1)}, bf16[512,256]{1,0:T(8,128)(2,1)S(1)}, u32[]{:S(2)}, u32[]{:S(2)}) collective-permute-start(bf16[512,256]{1,0:T(8,128)(2,1)S(1)} %get-tuple-element.174), channel_id=1, source_target_pairs={{0,8},{8,16},{16,24},{24,28},{28,20},{20,12},{12,4},{4,0},{1,9},{9... | collective-permute-start | bytes 786440 | tf_op jit(solution)/shard_map/ppermute | solution.py:350
  235.8 10.0 %collective-permute-start.42 = (bf16[512,256]{1,0:T(8,128)(2,1)S(1)}, bf16[512,256]{1,0:T(8,128)(2,1)S(1)}, u32[]{:S(2)}, u32[]{:S(2)}) collective-permute-start(bf16[512,256]{1,0:T(8,128)(2,1)S(1)} %get-tuple-element.175), channel_id=1, source_target_pairs={{0,4},{8,0},{16,8},{24,16},{28,24},{20,28},{12,20},{4,12},{1,5},{9... | collective-permute-start | bytes 786440 | tf_op jit(solution)/shard_map/ppermute | solution.py:350
  240.8 9.7 %collective-permute-start.37 = (bf16[512,256]{1,0:T(8,128)(2,1)S(1)}, bf16[512,256]{1,0:T(8,128)(2,1)S(1)}, u32[]{:S(2)}, u32[]{:S(2)}) collective-permute-start(bf16[512,256]{1,0:T(8,128)(2,1)S(1)} %get-tuple-element.172), channel_id=1, source_target_pairs={{0,8},{8,16},{16,24},{24,28},{28,20},{20,12},{12,4},{4,0},{1,9},{9... | collective-permute-start | bytes 786440 | tf_op jit(solution)/shard_map/ppermute | solution.py:350
  241.5 10.0 %collective-permute-start.38 = (bf16[512,256]{1,0:T(8,128)(2,1)S(1)}, bf16[512,256]{1,0:T(8,128)(2,1)S(1)}, u32[]{:S(2)}, u32[]{:S(2)}) collective-permute-start(bf16[512,256]{1,0:T(8,128)(2,1)S(1)} %get-tuple-element.173), channel_id=1, source_target_pairs={{0,4},{8,0},{16,8},{24,16},{28,24},{20,28},{12,20},{4,12},{1,5},{9... | collective-permute-start | bytes 786440 | tf_op jit(solution)/shard_map/ppermute | solution.py:350
  (60 other events, 569.8 us)
